TPU v7x, 128 devices: a whole 4x4x4 slice. The times are simulated.
128 devices in a mesh: lat: 8 (over x_lo, z), lon: 16 (over x_hi, y, core).
Axes of the slice: x: 4 (x_hi: 2, x_lo: 2; x = x_hi * 2 + x_lo), y: 4, z: 4, core: 2. Of those that a mesh axis runs over, the one named last changes fastest.
Arguments:
- wind_u: float32 [8, 512, 12000], P(None, 'lat', 'lon'), may hold values from -6 to 6
- wind_v: float32 [8, 512, 12000], P(None, 'lat', 'lon'), may hold values from -6 to 6
- tracer: float32 [8, 512, 12000], P(None, 'lat', 'lon'), may hold values from -6 to 6
- cutoff: int32 [512], P('lat'), may hold values from 1 to 1024, as said below
- row_scale: float32 [512], P('lat'), may hold values from 1 to 10
Outputs:
- tracer_next: float32 [8, 512, 12000], P(None, 'lat', 'lon')
- divergence: float32 [8, 512, 12000], P(None, 'lat', 'lon')
- vorticity: float32 [8, 512, 12000], P(None, 'lat', 'lon')
Inputs may be any that keep to these rules, and one draw needn't show every extreme that they name: cutoff of row r is min(1024, 1024 * (r + 1) // 512 + j) with a whole j from 0 to 63 drawn per row, and at least 1; the last row's is 1024.
All inputs are finite; a program needn't handle non-finite values.
Results may differ from a plain program's by a relative error of at most 0.00014.
Values sent between devices are 32-bit elements; how exact they have to be, the bound alone decides.
A program may use at most 128 MiB of HBM per device.

v0:
```python
import math

import jax
import jax.numpy as jnp
from jax import lax
from jax.sharding import PartitionSpec as P

NLON = 12000
KMAX = 1024
BLOCK = 128


courant = 0.5


def padded(cells, sides, width, closed):
    for axis, dim in sides:
        count = lax.axis_size(axis)
        ends = count if closed else count - 1
        head = lax.slice_in_dim(cells, 0, width, axis=dim)
        tail = lax.slice_in_dim(cells, cells.shape[dim] - width, cells.shape[dim], axis=dim)
        cells = jnp.concatenate(
            [
                lax.ppermute(tail, axis, [(i, (i + 1) % count) for i in range(ends)]),
                cells,
                lax.ppermute(head, axis, [((i + 1) % count, i) for i in range(ends)]),
            ],
            axis=dim,
        )
    return cells


def phase_tables(offset, count, first):
    positions = offset + jnp.arange(count, dtype=jnp.int32)
    numbers = first + jnp.arange(BLOCK, dtype=jnp.int32)
    turns = positions[:, None] * numbers[None, :] % NLON
    angles = turns.astype(jnp.float32) * (2.0 * math.pi / NLON)
    return (jnp.cos(angles), jnp.sin(angles))


def block_weights(limits, first):
    numbers = first + jnp.arange(BLOCK, dtype=jnp.int32)
    factor = jnp.where(numbers == 0, 1.0, 2.0).astype(jnp.float32) / NLON
    return jnp.where(numbers[None, :] < limits[:, None], factor[None, :], jnp.float32(0.0))


def contract_rows(coeffs, table):
    return lax.dot_general(
        coeffs,
        table,
        (((1,), (1,)), ((), ())),
        precision=lax.Precision.HIGHEST,
        preferred_element_type=jnp.float32,
    )


def analyse(lines, offset, blocks):
    count = lines.shape[1]
    empty = jnp.zeros((lines.shape[0], KMAX), jnp.float32)

    def analyse_step(index, carry):
        cosine, sine_part = carry
        first = index * BLOCK
        table_c, table_s = phase_tables(offset, count, first)
        part_c = jnp.dot(
            lines, table_c, precision=lax.Precision.HIGHEST, preferred_element_type=jnp.float32
        )
        part_s = jnp.dot(
            lines, table_s, precision=lax.Precision.HIGHEST, preferred_element_type=jnp.float32
        )
        return (
            lax.dynamic_update_slice_in_dim(cosine, part_c, first, 1),
            lax.dynamic_update_slice_in_dim(sine_part, part_s, first, 1),
        )

    return lax.fori_loop(0, blocks, analyse_step, (empty, empty))


def synthesise(cosine, sine_part, limits, offset, count, blocks):
    empty = jnp.zeros((cosine.shape[0], count), jnp.float32)

    def synthesise_step(index, carry):
        first = index * BLOCK
        table_c, table_s = phase_tables(offset, count, first)
        weights = block_weights(limits, first)
        coef_c = lax.dynamic_slice_in_dim(cosine, first, BLOCK, 1) * weights
        coef_s = lax.dynamic_slice_in_dim(sine_part, first, BLOCK, 1) * weights
        values = carry[0] + contract_rows(coef_c, table_c) + contract_rows(coef_s, table_s)
        return (values,)

    start = (empty,)
    return lax.fori_loop(0, blocks, synthesise_step, start)


def on_device(wind_u, wind_v, tracer, cutoff, row_scale):
    levels, rows, width = wind_u.shape
    lines = jnp.stack([wind_u, wind_v, tracer]).reshape(3 * levels * rows, width)
    blocks = (jnp.max(cutoff) + BLOCK - 1) // BLOCK
    moved = lax.all_to_all(lines, "lon", split_axis=0, concat_axis=1, tiled=True)
    share = moved.shape[0]
    line_ids = lax.axis_index("lon") * share + jnp.arange(share, dtype=jnp.int32)
    row_ids = line_ids % rows
    matches = row_ids[:, None] == jnp.arange(rows, dtype=jnp.int32)[None, :]
    limits = jnp.sum(jnp.where(matches, cutoff[None, :], 0), axis=1)
    cosine, sine_part = analyse(moved, 0, blocks)
    whole_rows = synthesise(cosine, sine_part, limits, 0, NLON, blocks)
    returned = lax.all_to_all(jnp.stack(whole_rows), "lon", split_axis=2, concat_axis=1, tiled=True)
    result = tuple((returned[number] for number in range(len(whole_rows))))
    filtered = result[0].reshape(3, levels, rows, width)
    padded_lon = padded(filtered, (("lon", 3),), 1, True)
    lon_change = padded_lon[..., 2:] - padded_lon[..., :-2]
    metric = row_scale[None, :, None]
    weighted = jnp.stack([filtered[0] / metric, filtered[1] / metric, filtered[2]])
    padded_lat = padded(weighted, (("lat", 2),), 1, False)
    lat_change = padded_lat[:, :, 2:] - padded_lat[:, :, :-2]
    divergence = metric * (lon_change[0] + lat_change[1])
    vorticity = metric * (lon_change[1] - lat_change[0])
    tracer_next = tracer - courant * (
        filtered[0] * metric * lon_change[2] + filtered[1] * lat_change[2]
    )
    return (tracer_next, divergence, vorticity)


def solution(mesh):
    in_specs = (
        P(None, "lat", "lon"),
        P(None, "lat", "lon"),
        P(None, "lat", "lon"),
        P("lat"),
        P("lat"),
    )
    out_specs = (P(None, "lat", "lon"), P(None, "lat", "lon"), P(None, "lat", "lon"))
    return jax.shard_map(
        on_device, mesh=mesh, in_specs=in_specs, out_specs=out_specs, check_vma=False
    )
```

profile of v0, /device:TPU:31, one launch (start us, length us, event | category | flops | bytes accessed | tf_op | source)
XLA Modules:
  0.0 1290.4 jit_solution(17541776767352156428)
XLA Ops:
  14.6 64.4 %all-to-all-done = f32[16,96,750]{2,1,0:T(8,128)} async-done(((f32[16,96,750]{2,1,0:T(8,128)}), f32[16,96,750]{2,1,0:T(8,128)}, u32[]{:S(2)}, u32[]{:S(2)}) %all-to-all-start) | async-done | bytes 4608032 | tf_op jit(solution)/shard_map/all_to_all | solution.py:99
  92.4 424.6 %while.26 = (s32[]{:T(128)}, f32[96,1024]{1,0:T(8,128)S(1)}, f32[96,1024]{1,0:T(8,128)S(1)}, s32[]{:T(128)}, f32[96,12000]{1,0:T(8,128)}, /*index=5*/s32[]{:T(128)}, s32[]{:T(128)}, s32[]{:T(128)}, s32[]{:T(128)}) while((s32[]{:T(128)}, f32[96,1024]{1,0:T(8,128)S(1)}, f32[96,1024]{1,0:T(8,128)S(1)}, s32[]{:T(128)}, f32[96,12000]{1,0:T(8,128)}, ...), condition=%wide.region_3.4_spmd, body=%wide.region_2.3_spmd.sunk | while | flops 3566592000 | bytes 27760316 | solution.py:76
  123.2 37.0 %fusion.102 = f32[96,1024]{1,0:T(8,128)S(1)} fusion(f32[96,1024]{1,0:T(8,128)S(1)} %get-tuple-element.273, s32[]{:T(128)S(6)} %select_n.125, f32[96,12000]{1,0:T(8,128)S(1)} %copy-done.3, s32[128]{0:T(128)S(1)} %iota_add_fusion.4), kind=kOutput, calls=%fused_computation.20.clone.1 | convolution fusion | flops 1783296000 | bytes 4669956 | tf_op jit(solution)/shard_map/while/body/dot_general | solution.py:68
  190.5 37.0 %fusion.102 = f32[96,1024]{1,0:T(8,128)S(1)} fusion(f32[96,1024]{1,0:T(8,128)S(1)} %get-tuple-element.273, s32[]{:T(128)S(6)} %select_n.125, f32[96,12000]{1,0:T(8,128)S(1)} %copy-done.3, s32[128]{0:T(128)S(1)} %iota_add_fusion.4), kind=kOutput, calls=%fused_computation.20.clone.1 | convolution fusion | flops 1783296000 | bytes 4669956 | tf_op jit(solution)/shard_map/while/body/dot_general | solution.py:68
  257.9 37.0 %fusion.102 = f32[96,1024]{1,0:T(8,128)S(1)} fusion(f32[96,1024]{1,0:T(8,128)S(1)} %get-tuple-element.273, s32[]{:T(128)S(6)} %select_n.125, f32[96,12000]{1,0:T(8,128)S(1)} %copy-done.3, s32[128]{0:T(128)S(1)} %iota_add_fusion.4), kind=kOutput, calls=%fused_computation.20.clone.1 | convolution fusion | flops 1783296000 | bytes 4669956 | tf_op jit(solution)/shard_map/while/body/dot_general | solution.py:68
  325.2 37.0 %fusion.102 = f32[96,1024]{1,0:T(8,128)S(1)} fusion(f32[96,1024]{1,0:T(8,128)S(1)} %get-tuple-element.273, s32[]{:T(128)S(6)} %select_n.125, f32[96,12000]{1,0:T(8,128)S(1)} %copy-done.3, s32[128]{0:T(128)S(1)} %iota_add_fusion.4), kind=kOutput, calls=%fused_computation.20.clone.1 | convolution fusion | flops 1783296000 | bytes 4669956 | tf_op jit(solution)/shard_map/while/body/dot_general | solution.py:68
  392.6 37.0 %fusion.102 = f32[96,1024]{1,0:T(8,128)S(1)} fusion(f32[96,1024]{1,0:T(8,128)S(1)} %get-tuple-element.273, s32[]{:T(128)S(6)} %select_n.125, f32[96,12000]{1,0:T(8,128)S(1)} %copy-done.3, s32[128]{0:T(128)S(1)} %iota_add_fusion.4), kind=kOutput, calls=%fused_computation.20.clone.1 | convolution fusion | flops 1783296000 | bytes 4669956 | tf_op jit(solution)/shard_map/while/body/dot_general | solution.py:68
  459.9 37.0 %fusion.102 = f32[96,1024]{1,0:T(8,128)S(1)} fusion(f32[96,1024]{1,0:T(8,128)S(1)} %get-tuple-element.273, s32[]{:T(128)S(6)} %select_n.125, f32[96,12000]{1,0:T(8,128)S(1)} %copy-done.3, s32[128]{0:T(128)S(1)} %iota_add_fusion.4), kind=kOutput, calls=%fused_computation.20.clone.1 | convolution fusion | flops 1783296000 | bytes 4669956 | tf_op jit(solution)/shard_map/while/body/dot_general | solution.py:68
  519.5 377.2 %while.27 = (s32[]{:T(128)}, f32[96,12000]{1,0:T(8,128)}, s32[]{:T(128)}, f32[96,1024]{1,0:T(8,128)S(1)}, s32[96]{0:T(128)S(1)}, /*index=5*/f32[96,1024]{1,0:T(8...) while((s32[]{:T(128)}, f32[96,12000]{1,0:T(8,128)}, s32[]{:T(128)}, f32[96,1024]{1,0:T(8,128)S(1)}, ...), condition=%wide.region_5.6_spmd, body=%wide.region_4.5_spmd.sunk | while | flops 3568970240 | bytes 18547884 | solution.py:92
  519.5 30.8 %convolution_add_fusion.4 = f32[96,12000]{1,0:T(8,128)S(1)} fusion(f32[96,12000]{1,0:T(8,128)} %get-tuple-element.300, s32[128]{0:T(128)S(1)} %iota_add_fusion.5, f32[96,1024]{1,0:T(8,128)S(1)} %get-tuple-element.312, s32[]{:T(128)S(6)} %select_n.131, f32[128]{0:T(128)S(1)} %fusion.105, s32[96]{0:T(128)S(1)} %get-tuple-element.313), kind=kOutput, calls=%fused_computation.29.clone.1 | convolution fusion | flops 1784484864 | bytes 9267204 | tf_op jit(solution)/shard_map/while/body/dot_general | solution.py:48
  550.3 30.7 %convolution_add_fusion.5 = f32[96,12000]{1,0:T(8,128)} fusion(f32[96,12000]{1,0:T(8,128)S(1)} %convolution_add_fusion.4, s32[128]{0:T(128)S(1)} %iota_add_fusion.5, f32[96,1024]{1,0:T(8,128)S(1)} %get-tuple-element.314, s32[]{:T(128)S(6)} %select_n.131, f32[128]{0:T(128)S(1)} %fusion.105, s32[96]{0:T(128)S(1)} %get-tuple-element.313), kind=kOutput, calls=%fused_computation.28.clone.1 | convolution fusion | flops 1784484864 | bytes 9279492 | tf_op jit(solution)/shard_map/while/body/dot_general | solution.py:48
  581.0 30.8 %convolution_add_fusion.4 = f32[96,12000]{1,0:T(8,128)S(1)} fusion(f32[96,12000]{1,0:T(8,128)} %get-tuple-element.300, s32[128]{0:T(128)S(1)} %iota_add_fusion.5, f32[96,1024]{1,0:T(8,128)S(1)} %get-tuple-element.312, s32[]{:T(128)S(6)} %select_n.131, f32[128]{0:T(128)S(1)} %fusion.105, s32[96]{0:T(128)S(1)} %get-tuple-element.313), kind=kOutput, calls=%fused_computation.29.clone.1 | convolution fusion | flops 1784484864 | bytes 9267204 | tf_op jit(solution)/shard_map/while/body/dot_general | solution.py:48
  611.8 30.7 %convolution_add_fusion.5 = f32[96,12000]{1,0:T(8,128)} fusion(f32[96,12000]{1,0:T(8,128)S(1)} %convolution_add_fusion.4, s32[128]{0:T(128)S(1)} %iota_add_fusion.5, f32[96,1024]{1,0:T(8,128)S(1)} %get-tuple-element.314, s32[]{:T(128)S(6)} %select_n.131, f32[128]{0:T(128)S(1)} %fusion.105, s32[96]{0:T(128)S(1)} %get-tuple-element.313), kind=kOutput, calls=%fused_computation.28.clone.1 | convolution fusion | flops 1784484864 | bytes 9279492 | tf_op jit(solution)/shard_map/while/body/dot_general | solution.py:48
  642.5 30.8 %convolution_add_fusion.4 = f32[96,12000]{1,0:T(8,128)S(1)} fusion(f32[96,12000]{1,0:T(8,128)} %get-tuple-element.300, s32[128]{0:T(128)S(1)} %iota_add_fusion.5, f32[96,1024]{1,0:T(8,128)S(1)} %get-tuple-element.312, s32[]{:T(128)S(6)} %select_n.131, f32[128]{0:T(128)S(1)} %fusion.105, s32[96]{0:T(128)S(1)} %get-tuple-element.313), kind=kOutput, calls=%fused_computation.29.clone.1 | convolution fusion | flops 1784484864 | bytes 9267204 | tf_op jit(solution)/shard_map/while/body/dot_general | solution.py:48
  673.3 30.7 %convolution_add_fusion.5 = f32[96,12000]{1,0:T(8,128)} fusion(f32[96,12000]{1,0:T(8,128)S(1)} %convolution_add_fusion.4, s32[128]{0:T(128)S(1)} %iota_add_fusion.5, f32[96,1024]{1,0:T(8,128)S(1)} %get-tuple-element.314, s32[]{:T(128)S(6)} %select_n.131, f32[128]{0:T(128)S(1)} %fusion.105, s32[96]{0:T(128)S(1)} %get-tuple-element.313), kind=kOutput, calls=%fused_computation.28.clone.1 | convolution fusion | flops 1784484864 | bytes 9279492 | tf_op jit(solution)/shard_map/while/body/dot_general | solution.py:48
  704.1 30.8 %convolution_add_fusion.4 = f32[96,12000]{1,0:T(8,128)S(1)} fusion(f32[96,12000]{1,0:T(8,128)} %get-tuple-element.300, s32[128]{0:T(128)S(1)} %iota_add_fusion.5, f32[96,1024]{1,0:T(8,128)S(1)} %get-tuple-element.312, s32[]{:T(128)S(6)} %select_n.131, f32[128]{0:T(128)S(1)} %fusion.105, s32[96]{0:T(128)S(1)} %get-tuple-element.313), kind=kOutput, calls=%fused_computation.29.clone.1 | convolution fusion | flops 1784484864 | bytes 9267204 | tf_op jit(solution)/shard_map/while/body/dot_general | solution.py:48
  734.8 30.7 %convolution_add_fusion.5 = f32[96,12000]{1,0:T(8,128)} fusion(f32[96,12000]{1,0:T(8,128)S(1)} %convolution_add_fusion.4, s32[128]{0:T(128)S(1)} %iota_add_fusion.5, f32[96,1024]{1,0:T(8,128)S(1)} %get-tuple-element.314, s32[]{:T(128)S(6)} %select_n.131, f32[128]{0:T(128)S(1)} %fusion.105, s32[96]{0:T(128)S(1)} %get-tuple-element.313), kind=kOutput, calls=%fused_computation.28.clone.1 | convolution fusion | flops 1784484864 | bytes 9279492 | tf_op jit(solution)/shard_map/while/body/dot_general | solution.py:48
  765.6 30.8 %convolution_add_fusion.4 = f32[96,12000]{1,0:T(8,128)S(1)} fusion(f32[96,12000]{1,0:T(8,128)} %get-tuple-element.300, s32[128]{0:T(128)S(1)} %iota_add_fusion.5, f32[96,1024]{1,0:T(8,128)S(1)} %get-tuple-element.312, s32[]{:T(128)S(6)} %select_n.131, f32[128]{0:T(128)S(1)} %fusion.105, s32[96]{0:T(128)S(1)} %get-tuple-element.313), kind=kOutput, calls=%fused_computation.29.clone.1 | convolution fusion | flops 1784484864 | bytes 9267204 | tf_op jit(solution)/shard_map/while/body/dot_general | solution.py:48
  796.4 30.7 %convolution_add_fusion.5 = f32[96,12000]{1,0:T(8,128)} fusion(f32[96,12000]{1,0:T(8,128)S(1)} %convolution_add_fusion.4, s32[128]{0:T(128)S(1)} %iota_add_fusion.5, f32[96,1024]{1,0:T(8,128)S(1)} %get-tuple-element.314, s32[]{:T(128)S(6)} %select_n.131, f32[128]{0:T(128)S(1)} %fusion.105, s32[96]{0:T(128)S(1)} %get-tuple-element.313), kind=kOutput, calls=%fused_computation.28.clone.1 | convolution fusion | flops 1784484864 | bytes 9279492 | tf_op jit(solution)/shard_map/while/body/dot_general | solution.py:48
  827.1 30.8 %convolution_add_fusion.4 = f32[96,12000]{1,0:T(8,128)S(1)} fusion(f32[96,12000]{1,0:T(8,128)} %get-tuple-element.300, s32[128]{0:T(128)S(1)} %iota_add_fusion.5, f32[96,1024]{1,0:T(8,128)S(1)} %get-tuple-element.312, s32[]{:T(128)S(6)} %select_n.131, f32[128]{0:T(128)S(1)} %fusion.105, s32[96]{0:T(128)S(1)} %get-tuple-element.313), kind=kOutput, calls=%fused_computation.29.clone.1 | convolution fusion | flops 1784484864 | bytes 9267204 | tf_op jit(solution)/shard_map/while/body/dot_general | solution.py:48
  857.9 30.7 %convolution_add_fusion.5 = f32[96,12000]{1,0:T(8,128)} fusion(f32[96,12000]{1,0:T(8,128)S(1)} %convolution_add_fusion.4, s32[128]{0:T(128)S(1)} %iota_add_fusion.5, f32[96,1024]{1,0:T(8,128)S(1)} %get-tuple-element.314, s32[]{:T(128)S(6)} %select_n.131, f32[128]{0:T(128)S(1)} %fusion.105, s32[96]{0:T(128)S(1)} %get-tuple-element.313), kind=kOutput, calls=%fused_computation.28.clone.1 | convolution fusion | flops 1784484864 | bytes 9279492 | tf_op jit(solution)/shard_map/while/body/dot_general | solution.py:48
  902.9 77.6 %all_to_all.34 = f32[1,96,12000]{1,0,2:T(1,128)} all-to-all(f32[1,96,12000]{1,0,2:T(1,128)} %bitcast.58), channel_id=1, replica_groups=mesh['lat'=8,'lon'=16] {'lon'}, dimensions={2} | all-to-all | bytes 9216000 | tf_op jit(solution)/shard_map/all_to_all | solution.py:107
  1017.8 132.4 %collective-permute-start.3 = (f32[3,8,1,750]{3,2,1,0:T(1,128)S(1)}, f32[3,8,1,750]{3,2,1,0:T(1,128)S(1)}, u32[]{:S(2)}, u32[]{:S(2)}) collective-permute-start(f32[3,8,1,750]{3,2,1,0:T(1,128)S(1)} %get-tuple-element.190), channel_id=1, source_target_pairs={{0,16},{16,32},{32,48},{48,64},{64,80},{80,96},{96,112},{1,17},{17... | collective-permute-start | bytes 216008 | tf_op jit(solution)/shard_map/ppermute | solution.py:24
  1160.4 123.9 %collective-permute-done.2 = f32[3,8,1,750]{3,2,1,0:T(1,128)S(1)} collective-permute-done((f32[3,8,1,750]{3,2,1,0:T(1,128)S(1)}, f32[3,8,1,750]{3,2,1,0:T(1,128)S(1)}, u32[]{:S(2)}, u32[]{:S(2)}) %collective-permute-start.2) | collective-permute-done | bytes 72032 | tf_op jit(solution)/shard_map/ppermute | solution.py:26
  (81 shorter events, 270.8 us)
Async XLA Ops:
  5.6 7.5 copy-start.5
  5.6 73.3 %all-to-all-start = ((f32[16,96,750]{2,1,0:T(8,128)}), f32[16,96,750]{2,1,0:T(8,128)}, u32[]{:S(2)}, u32[]{:S(2)}) async-start(f32[16,96,750]{2,1,0:T(8,128)} %bitcast.59), calls=%async_computation | async-start | bytes 9437184 | tf_op jit(solution)/shard_map/all_to_all | solution.py:99
  92.9 30.3 %copy-start.3 = (f32[96,12000]{1,0:T(8,128)S(1)}, f32[96,12000]{1,0:T(8,128)}, u32[]{:S(2)}) copy-start(f32[96,12000]{1,0:T(8,128)} %get-tuple-element.284) | copy-start | bytes 13824004 | tf_op jit(solution)/shard_map/while
  160.2 30.3 %copy-start.3 = (f32[96,12000]{1,0:T(8,128)S(1)}, f32[96,12000]{1,0:T(8,128)}, u32[]{:S(2)}) copy-start(f32[96,12000]{1,0:T(8,128)} %get-tuple-element.284) | copy-start | bytes 13824004 | tf_op jit(solution)/shard_map/while
  227.5 30.3 %copy-start.3 = (f32[96,12000]{1,0:T(8,128)S(1)}, f32[96,12000]{1,0:T(8,128)}, u32[]{:S(2)}) copy-start(f32[96,12000]{1,0:T(8,128)} %get-tuple-element.284) | copy-start | bytes 13824004 | tf_op jit(solution)/shard_map/while
  294.9 30.3 %copy-start.3 = (f32[96,12000]{1,0:T(8,128)S(1)}, f32[96,12000]{1,0:T(8,128)}, u32[]{:S(2)}) copy-start(f32[96,12000]{1,0:T(8,128)} %get-tuple-element.284) | copy-start | bytes 13824004 | tf_op jit(solution)/shard_map/while
  362.2 30.3 %copy-start.3 = (f32[96,12000]{1,0:T(8,128)S(1)}, f32[96,12000]{1,0:T(8,128)}, u32[]{:S(2)}) copy-start(f32[96,12000]{1,0:T(8,128)} %get-tuple-element.284) | copy-start | bytes 13824004 | tf_op jit(solution)/shard_map/while
  429.6 30.3 %copy-start.3 = (f32[96,12000]{1,0:T(8,128)S(1)}, f32[96,12000]{1,0:T(8,128)}, u32[]{:S(2)}) copy-start(f32[96,12000]{1,0:T(8,128)} %get-tuple-element.284) | copy-start | bytes 13824004 | tf_op jit(solution)/shard_map/while
  1001.4 6.5 copy-start.4
  1006.5 3.6 copy-start
  1011.6 140.5 %collective-permute-start.1 = (f32[3,8,64,1]{2,1,3,0:T(8,128)S(1)}, f32[3,8,64,1]{2,1,3,0:T(8,128)S(1)}, u32[]{:S(2)}, u32[]{:S(2)}) collective-permute-start(f32[3,8,64,1]{2,1,3,0:T(8,128)S(1)} %copy.35), channel_id=1, source_target_pairs={{0,1},{1,2},{2,3},{3,4},{4,5},{5,6},{6,7},{7,8},{8,9},{9,10},{10,1... | collective-permute-start | bytes 18440 | tf_op jit(solution)/shard_map/ppermute | solution.py:24
  1016.4 136.1 %collective-permute-start = (f32[3,8,64,1]{2,1,3,0:T(8,128)S(1)}, f32[3,8,64,1]{2,1,3,0:T(8,128)S(1)}, u32[]{:S(2)}, u32[]{:S(2)}) collective-permute-start(f32[3,8,64,1]{2,1,3,0:T(8,128)S(1)} %copy.33), channel_id=1, source_target_pairs={{1,0},{2,1},{3,2},{4,3},{5,4},{6,5},{7,6},{8,7},{9,8},{10,9},{11,1... | collective-permute-start | bytes 18440 | tf_op jit(solution)/shard_map/ppermute | solution.py:26
  1017.8 142.7 %collective-permute-start.3 = (f32[3,8,1,750]{3,2,1,0:T(1,128)S(1)}, f32[3,8,1,750]{3,2,1,0:T(1,128)S(1)}, u32[]{:S(2)}, u32[]{:S(2)}) collective-permute-start(f32[3,8,1,750]{3,2,1,0:T(1,128)S(1)} %get-tuple-element.190), channel_id=1, source_target_pairs={{0,16},{16,32},{32,48},{48,64},{64,80},{80,96},{96,112},{1,17},{17... | collective-permute-start | bytes 216008 | tf_op jit(solution)/shard_map/ppermute | solution.py:24
  1150.2 134.1 %collective-permute-start.2 = (f32[3,8,1,750]{3,2,1,0:T(1,128)S(1)}, f32[3,8,1,750]{3,2,1,0:T(1,128)S(1)}, u32[]{:S(2)}, u32[]{:S(2)}) collective-permute-start(f32[3,8,1,750]{3,2,1,0:T(1,128)S(1)} %get-tuple-element.189), channel_id=1, source_target_pairs={{16,0},{32,16},{48,32},{64,48},{80,64},{96,80},{112,96},{17,1},{33... | collective-permute-start | bytes 216008 | tf_op jit(solution)/shard_map/ppermute | solution.py:26
  1152.5 133.4 %slice-start = ((s8[4718592]{0:T(1024)(128)(4,1)}), s8[524288]{0:T(1024)(128)(4,1)S(1)}, s32[]{:S(2)}) async-start(s8[4718592]{0:T(1024)(128)(4,1)} %bitcast.55), calls=%async_computation.2 | async-start | bytes 1048576
  1153.7 130.6 %copy-start.1 = (f32[1,8,64,750]{3,2,1,0:T(8,128)S(1)}, f32[1,8,64,750]{3,2,1,0:T(8,128)}, u32[]{:S(2)}) copy-start(f32[1,8,64,750]{3,2,1,0:T(8,128)} %get-tuple-element.186) | copy-start | bytes 4608004
  1153.7 130.6 %copy-start.2 = (f32[1,8,64,750]{3,2,1,0:T(8,128)S(1)}, f32[1,8,64,750]{3,2,1,0:T(8,128)}, u32[]{:S(2)}) copy-start(f32[1,8,64,750]{3,2,1,0:T(8,128)} %get-tuple-element.191) | copy-start | bytes 4608004
  1153.7 132.2 %slice-start.1 = ((s8[4718592]{0:T(1024)(128)(4,1)}), s8[4194304]{0:T(1024)(128)(4,1)S(1)}, s32[]{:S(2)}) async-start(s8[4718592]{0:T(1024)(128)(4,1)} %bitcast.55), calls=%async_computation.3 | async-start | bytes 8388608
where the time goes:
time: 1300 us; the launch traced here: 1290 us
  matrix products  773 us (59%)
  waiting for transfers between devices  188 us (14%)
  starting transfers between devices  146 us (11%)
  blocking collectives  77.6 us (6%)
  local copies, waits for them, and re-layouts  53 us (4%)
  loops' own time  29.1 us (2%)
  other arithmetic  21.9 us (2%)
    dot_general x12, matrix products, contract_rows(): lax.dot_general(coeffs, table, (((1,), (1,)), ((), ())), precision=lax.Pr...  369 us
    dot_general x6, matrix products, analyse_step(): jnp.dot(lines, table_s, precision=lax.Precision.HIGHEST, preferred_elemen...  222 us
    dot_general x6, matrix products, analyse_step(): jnp.dot(lines, table_c, precision=lax.Precision.HIGHEST, preferred_elemen...  182 us
    ppermute x2, starting transfers between devices, padded(): lax.ppermute(tail, axis, [(i, (i + 1) % count) for i in range(ends)])  137 us
    ppermute x2, waiting for transfers between devices, padded(): lax.ppermute(head, axis, [((i + 1) % count, i) for i in range(ends)])  124 us
    all_to_all x1, blocking collectives, on_device(): lax.all_to_all(jnp.stack(whole_rows), 'lon', split_axis=2, concat_axis=1,...  77.6 us
    all_to_all x1, waiting for transfers between devices, on_device(): lax.all_to_all(lines, 'lon', split_axis=0, concat_axis=1, tiled=True)  64.4 us
    all_to_all x3, local copies, waits for them, and re-layouts, on_device(): lax.all_to_all(jnp.stack(whole_rows), 'lon', split_axis=2, concat_axis=1,...  26.1 us
  transfers between devices with their start and end apart: 5, of which 2 were waited for; matrix products, arithmetic and copies ran while one was open for 1% of the time, Pallas kernels for 0%

commit v1 on v0

v1 whole, which is shorter than its diff:
```python
import functools
import math

import numpy as np
import jax
import jax.numpy as jnp
from jax import lax
from jax.experimental import pallas as pl
from jax.experimental.pallas import tpu as pltpu
from jax.sharding import PartitionSpec as P

NLON = 12000
SEG = 750
PAD = 768
LANES = 128
MESH = pl.DeviceIdType.MESH
F32 = jnp.float32
BF16 = jnp.bfloat16
ROOT_HALF = math.sqrt(0.5)
courant = 0.5


def phase(steps):
    angle = 2.0 * np.pi * (np.asarray(steps, dtype=np.int64) % NLON) / NLON
    return np.stack([np.cos(angle), np.sin(angle)]).astype(np.float32)


def small_tables():
    k2 = np.arange(128)
    start = (750 * np.arange(2)[:, None] + 32 * np.arange(24)[None, :]).reshape(48)
    inner = np.arange(32)
    last = np.where(inner == 31, -1 - 736, inner)
    coarse, fine = [], []
    for mult in (8 * k2, 8 * k2 + 4):
        coarse.append(phase(start[:, None] * mult[None, :]))
        fine.append(np.stack([phase(b[:, None] * mult[None, :]) for b in (inner, last)]))
    lanes = np.arange(PAD)
    lanes = np.where(lanes == PAD - 1, -1, lanes)
    place = 750 * np.arange(2)[:, None] + lanes[None, :]
    twiddle = np.stack([phase(k1 * place) for k1 in (1, 2, 3)])
    return np.stack(coarse), np.stack(fine), twiddle[:, :, :, None, :]


def split(values):
    high = values.astype(BF16)
    return high, (values - high.astype(F32)).astype(BF16)


def dot3(high, low, table_high, table_low, dims):
    def one(a, b):
        return lax.dot_general(a, b, (dims, ((), ())), preferred_element_type=F32)

    return one(high, table_high) + (one(high, table_low) + one(low, table_high))


def filter_kernel(
    u_ref, v_ref, q_ref, cut_ref, scale_ref, coarse_ref, fine_ref, tw_ref,
    filt_ref, edge_ref,
    raw, table_h, table_l, y_h, y_l, prod, zed, back, edge_out,
    fs, fr, bs, br, es, er, loc,
):
    lat = lax.axis_index("lat")
    me = lax.axis_index("lon")
    row_group, level_half = me % 8, me // 8
    fields = (u_ref, v_ref, q_ref)

    def block_of(ref, member):
        return ref.at[pl.ds(4 * (member // 8), 4), pl.ds(pl.multiple_of(8 * (member % 8), 8), 8)]

    def forward(f, i):
        dest = (me + i) % 16
        return pltpu.make_async_remote_copy(
            src_ref=block_of(fields[f], dest), dst_ref=raw.at[f, me],
            send_sem=fs.at[f, i], recv_sem=fr.at[f, i],
            device_id={"lon": dest}, device_id_type=MESH,
        )

    def own_forward(f):
        return pltpu.make_async_copy(block_of(fields[f], me), raw.at[f, me], loc.at[f])

    def backward(f, i):
        dest = (me + i) % 16
        return pltpu.make_async_remote_copy(
            src_ref=back.at[f, dest], dst_ref=block_of(filt_ref.at[f], me),
            send_sem=bs.at[f, i], recv_sem=br.at[f, i],
            device_id={"lon": dest}, device_id_type=MESH,
        )

    def own_backward(f):
        return pltpu.make_async_copy(back.at[f, me], block_of(filt_ref.at[f], me), loc.at[3 + f])

    def edge(f, side, i):
        dest = (me + i) % 16
        return pltpu.make_async_remote_copy(
            src_ref=edge_out.at[f, dest], dst_ref=edge_ref.at[f, side, pl.ds(4 * level_half, 4)],
            send_sem=es.at[f, i], recv_sem=er.at[f, side, level_half],
            device_id={"lat": lat + (1 - 2 * side), "lon": dest}, device_id_type=MESH,
        )

    sends_down = jnp.logical_and(row_group == 7, lat < 7)
    sends_up = jnp.logical_and(row_group == 0, lat > 0)

    for f in range(3):
        own_forward(f).start()

        def start(i, carry, f=f):
            forward(f, i).start()
            return carry

        lax.fori_loop(1, 16, start, 0)

    for kind in range(2):
        for c in range(2):
            def fill(a, carry, kind=kind, c=c):
                tail = jnp.where(a == 23, 1, 0)
                c1 = coarse_ref[kind, 0, pl.ds(24 * c + a, 1), :]
                s1 = coarse_ref[kind, 1, pl.ds(24 * c + a, 1), :]
                c2 = fine_ref[kind, tail, 0]
                s2 = fine_ref[kind, tail, 1]
                rows = pl.ds(pl.multiple_of(32 * a, 32), 32)
                for side, value in enumerate((c1 * c2 - s1 * s2, s1 * c2 + c1 * s2)):
                    high, low = split(value)
                    cols = pl.ds(128 * side, 128)
                    table_h[kind, c, rows, cols] = high
                    table_l[kind, c, rows, cols] = low
                return carry

            lax.fori_loop(0, 24, fill, 0)
    y_h[...] = jnp.zeros_like(y_h)
    y_l[...] = jnp.zeros_like(y_l)

    row_at = lax.broadcasted_iota(jnp.int32, (8, 256), 0)
    limits = jnp.zeros((8, 256), jnp.int32)
    for row in range(8):
        limits = jnp.where(row_at == row, cut_ref[8 * row_group + row], limits)
    k2 = lax.broadcasted_iota(jnp.int32, (8, 256), 1) % 128
    sign = jnp.where(lax.broadcasted_iota(jnp.int32, (8, 256), 1) < 128, 1.0, -1.0).astype(F32)
    weight = 2.0 / NLON

    def kept(k):
        return jnp.where(k < limits, F32(weight), F32(0.0))

    for f in range(3):
        own_forward(f).wait()

        def arrive(i, carry, f=f):
            forward(f, i).wait_recv()
            return carry

        lax.fori_loop(1, 16, arrive, 0)

        def analyse(pair, carry, f=f):
            lines = pl.ds(pl.multiple_of(16 * pair, 16), 16)
            for c in range(2):
                for lo in range(0, SEG, LANES):
                    hi = min(SEG, lo + LANES)
                    x = [
                        raw[f, 2 * d + c, pl.ds(2 * pair, 2), :, lo:hi].reshape(16, hi - lo)
                        for d in range(8)
                    ]
                    s = [x[d] + x[d + 4] for d in range(4)]
                    t = [x[d] - x[d + 4] for d in range(4)]
                    s02, s13 = s[0] + s[2], s[1] + s[3]
                    minus, plus = (t[3] - t[1]) * ROOT_HALF, (t[1] + t[3]) * -ROOT_HALF
                    parts = (
                        (t[0] + minus, -t[2] - plus),
                        (s[0] - s[2], s[1] - s[3]),
                        (t[0] - minus, t[2] - plus),
                    )
                    rows = [s02 - s13]
                    for k1 in range(3):
                        re, im = parts[k1]
                        co = tw_ref[k1, 0, c, :, lo:hi]
                        si = tw_ref[k1, 1, c, :, lo:hi]
                        rows += [re * co + im * si, im * co - re * si]
                    rows.append(s02 + s13)
                    for r, value in enumerate(rows):
                        high, low = split(value)
                        y_h[c, r, lines, lo:hi] = high
                        y_l[c, r, lines, lo:hi] = low
            return carry

        lax.fori_loop(0, 2, analyse, 0)

        for kind, r0, r1 in ((1, 0, 7), (0, 7, 8)):
            total = None
            for c in range(2):
                part = dot3(
                    y_h[c, r0:r1].reshape((r1 - r0) * 32, PAD), y_l[c, r0:r1].reshape((r1 - r0) * 32, PAD),
                    table_h[kind, c], table_l[kind, c], ((1,), (0,)),
                )
                total = part if total is None else total + part
            prod[r0:r1] = total.reshape(r1 - r0, 32, 256)

        def keep(level, carry):
            lines = pl.ds(pl.multiple_of(8 * level, 8), 8)
            zero = jnp.where(k2 == 0, F32(0.5), F32(1.0))
            prod[0, lines, :] = prod[0, lines, :] * kept(8 * k2 + 4)
            prod[7, lines, :] = prod[7, lines, :] * (kept(8 * k2) * zero)
            for k1 in (1, 2, 3):
                above, below = kept(8 * k2 + 4 + k1), kept(8 * k2 + 4 - k1)
                both, odd = above + below, (above - below) * sign
                r1, r2 = prod[2 * k1 - 1, lines, :], prod[2 * k1, lines, :]
                swap1 = jnp.concatenate([r1[:, 128:], r1[:, :128]], axis=1)
                swap2 = jnp.concatenate([r2[:, 128:], r2[:, :128]], axis=1)
                prod[2 * k1 - 1, lines, :] = both * r1 + odd * swap2
                prod[2 * k1, lines, :] = both * r2 - odd * swap1
            return carry

        lax.fori_loop(0, 4, keep, 0)

        for kind, r0, r1 in ((1, 0, 7), (0, 7, 8)):
            high, low = split(prod[r0:r1].reshape((r1 - r0) * 32, 256))
            for c in range(2):
                zed[c, r0:r1] = dot3(
                    high, low, table_h[kind, c], table_l[kind, c], ((1,), (1,))
                ).reshape(r1 - r0, 32, PAD)

        def synthesise(level, carry, f=f):
            lines = pl.ds(pl.multiple_of(8 * level, 8), 8)
            for c in range(2):
                for lo in range(0, PAD, LANES):
                    hi = lo + LANES
                    z = [zed[c, r, lines, lo:hi] for r in range(8)]
                    v = []
                    for k1 in range(3):
                        co = tw_ref[k1, 0, c, :, lo:hi]
                        si = tw_ref[k1, 1, c, :, lo:hi]
                        re, im = z[2 * k1 + 1], z[2 * k1 + 2]
                        v.append((re * co - im * si, im * co + re * si))
                    (ar, ai), (br_, bi), (cr, ci) = v
                    up, down = z[0] + z[7], z[0] - z[7]
                    even = (up + br_, down - bi, up - br_, down + bi)
                    p, m = (ar - cr) * ROOT_HALF, (ai + ci) * ROOT_HALF
                    odd = (ar + cr, p - m, ci - ai, -p - m)
                    for d in range(4):
                        one, other = even[d] + odd[d], even[d] - odd[d]
                        back[f, 2 * d + c, level, :, lo:hi] = one if d % 2 == 0 else -one
                        back[f, 2 * d + 8 + c, level, :, lo:hi] = other if d % 2 == 0 else -other
            return carry

        lax.fori_loop(0, 4, synthesise, 0)

        own_backward(f).start()

        def send(i, carry, f=f):
            backward(f, i).start()
            return carry

        lax.fori_loop(1, 16, send, 0)

        for side, sends, row in ((0, sends_down, 7), (1, sends_up, 0)):
            @pl.when(sends)
            def _(f=f, side=side, row=row):
                factor = 1.0 / jnp.full((1, PAD), scale_ref[8 * row_group + row], F32) if f < 2 else None

                def pack(member, carry):
                    for level in range(4):
                        value = back[f, member, level, row:row + 1, :]
                        edge_out[f, member, level] = value if factor is None else value * factor
                    return carry

                lax.fori_loop(0, 16, pack, 0)

                def post(i, carry):
                    edge(f, side, i).start()
                    return carry

                lax.fori_loop(0, 16, post, 0)

    for f in range(3):
        own_backward(f).wait()

        def finish(i, carry, f=f):
            forward(f, i).wait_send()
            backward(f, i).wait_send()
            backward(f, i).wait_recv()
            return carry

        lax.fori_loop(1, 16, finish, 0)
        for side, sends, gets in ((0, sends_down, lat > 0), (1, sends_up, lat < 7)):
            @pl.when(sends)
            def _(f=f, side=side):
                def sent(i, carry):
                    edge(f, side, i).wait_send()
                    return carry

                lax.fori_loop(0, 16, sent, 0)

            @pl.when(gets)
            def _(f=f, side=side):
                for half in range(2):
                    pltpu.make_async_remote_copy(
                        src_ref=edge_out.at[f, 0], dst_ref=edge_ref.at[f, side, pl.ds(4 * half, 4)],
                        send_sem=es.at[f, 0], recv_sem=er.at[f, side, half],
                        device_id={"lat": lat, "lon": (me + 1) % 16}, device_id_type=MESH,
                    ).wait_recv()


def stencil_kernel(filt_ref, edge_ref, tracer_ref, row_scale_ref, t_ref, d_ref, z_ref, scale_ref, inv_ref):
    lat = lax.axis_index("lat")

    @pl.when(pl.program_id(0) == 0)
    def _():
        def spread(row, carry):
            scale_ref[pl.ds(row, 1), :] = jnp.full((1, LANES), row_scale_ref[row], F32)
            return carry

        lax.fori_loop(0, 64, spread, 0, unroll=8)
        inv_ref[...] = 1.0 / scale_ref[...]

    scale = jnp.concatenate([scale_ref[...]] * (PAD // LANES), axis=1)
    inv = jnp.concatenate([inv_ref[...]] * (PAD // LANES), axis=1)
    first = lax.broadcasted_iota(jnp.int32, (64, PAD), 0) == 0
    last = lax.broadcasted_iota(jnp.int32, (64, PAD), 0) == 63

    def change(field, values):
        above = jnp.where(lat > 0, edge_ref[field, 0, 0], F32(0.0))
        below = jnp.where(lat < 7, edge_ref[field, 1, 0], F32(0.0))
        north = jnp.where(first, above, pltpu.roll(values, 1, 0))
        south = jnp.where(last, below, pltpu.roll(values, 63, 0))
        return south - north

    def east_west(values):
        return pltpu.roll(values, PAD - 1, 1) - pltpu.roll(values, 1, 1)

    u, v, q = filt_ref[0, 0], filt_ref[1, 0], filt_ref[2, 0]
    d_ref[0] = (scale * (east_west(u) + change(1, v * inv)))[:, :SEG]
    z_ref[0] = (scale * (east_west(v) - change(0, u * inv)))[:, :SEG]
    flux = u * scale * east_west(q) + v * change(2, q)
    t_ref[0] = tracer_ref[0] - courant * flux[:, :SEG]


def on_device(tables, wind_u, wind_v, tracer, cutoff, row_scale):
    coarse, fine, twiddle = (jnp.asarray(t) for t in tables)
    hbm = pl.BlockSpec(memory_space=pl.ANY)
    vmem = pl.BlockSpec(memory_space=pltpu.VMEM)
    smem = pl.BlockSpec(memory_space=pltpu.SMEM)
    dma = pltpu.SemaphoreType.DMA
    filt, edge = pl.pallas_call(
        filter_kernel,
        name="polar_filter",
        out_shape=(
            jax.ShapeDtypeStruct((3, 8, 64, PAD), F32),
            jax.ShapeDtypeStruct((3, 2, 8, 1, PAD), F32),
        ),
        in_specs=[hbm, hbm, hbm, smem, smem, vmem, vmem, vmem],
        out_specs=(hbm, hbm),
        scratch_shapes=[
            pltpu.VMEM((3, 16, 4, 8, SEG), F32),
            pltpu.VMEM((2, 2, PAD, 256), BF16),
            pltpu.VMEM((2, 2, PAD, 256), BF16),
            pltpu.VMEM((2, 8, 32, PAD), BF16),
            pltpu.VMEM((2, 8, 32, PAD), BF16),
            pltpu.VMEM((8, 32, 256), F32),
            pltpu.VMEM((2, 8, 32, PAD), F32),
            pltpu.VMEM((3, 16, 4, 8, PAD), F32),
            pltpu.VMEM((3, 16, 4, 1, PAD), F32),
            dma((3, 16)), dma((3, 16)), dma((3, 16)), dma((3, 16)),
            dma((3, 16)), dma((3, 2, 2)), dma((6,)),
        ],
        compiler_params=pltpu.CompilerParams(has_side_effects=True, vmem_limit_bytes=60 * 1024 * 1024),
    )(wind_u, wind_v, tracer, cutoff, row_scale, coarse, fine, twiddle)
    level = pl.BlockSpec((1, 64, SEG), lambda k: (k, 0, 0))
    shape = jax.ShapeDtypeStruct((8, 64, SEG), F32)
    return pl.pallas_call(
        stencil_kernel,
        name="flux_stencil",
        grid=(8,),
        out_shape=(shape, shape, shape),
        in_specs=[
            pl.BlockSpec((3, 1, 64, PAD), lambda k: (0, k, 0, 0)),
            pl.BlockSpec((3, 2, 1, 1, PAD), lambda k: (0, 0, k, 0, 0)),
            level, smem,
        ],
        out_specs=(level, level, level),
        scratch_shapes=[pltpu.VMEM((64, LANES), F32), pltpu.VMEM((64, LANES), F32)],
    )(filt, edge, tracer, row_scale)


def solution(mesh):
    in_specs = (
        P(None, "lat", "lon"),
        P(None, "lat", "lon"),
        P(None, "lat", "lon"),
        P("lat"),
        P("lat"),
    )
    out_specs = (P(None, "lat", "lon"), P(None, "lat", "lon"), P(None, "lat", "lon"))
    return jax.shard_map(
        functools.partial(on_device, small_tables()),
        mesh=mesh, in_specs=in_specs, out_specs=out_specs, check_vma=False,
    )
```

time: 1300 us -> 144 us (0.11)
  the two profiles are of different devices: /device:TPU:31 before, /device:TPU:19 now
where the time goes in v1:
time: 144 us
  Pallas kernels  143 us (99%)
    pallas_call x1, Pallas kernels, on_device(): pl.pallas_call(filter_kernel, name='polar_filter', out_shape=(jax.ShapeDt...  135 us
    pallas_call x1, Pallas kernels, on_device(): pl.pallas_call(stencil_kernel, name='flux_stencil', grid=(8,), out_shape=...  8.32 us

profile of v1, /device:TPU:19, one launch (start us, length us, event | category | flops | bytes accessed | tf_op | source)
XLA Modules:
  0.0 144.0 jit_solution(13494469083322575372)
XLA Ops:
  0.6 135.0 %polar_filter.1 = (f32[3,8,64,768]{3,2,1,0:T(8,128)}, f32[3,2,8,1,768]{4,3,2,1,0:T(1,128)}) custom-call(f32[8,64,750]{2,1,0:T(8,128)} %u_ref.1, f32[8,64,750]{2,1,0:T(8,128)} %v_ref.1, f32[8,64,750]{2,1,0:T(8,128)} %tracer_ref.1, s32[64]{0:T(128)} %cut_ref.1, f32[64]{0:T(128)} %row_scale_ref.1, f32[2,2,48,128]{3,2,1,0:T(8,128)} %constant.6.clone.coarse_ref, ...), custom_call_target="tpu_custom_call" | custom-call | tf_op jit(solution)/shard_map/polar_filter/pallas_call | solution.py:340
  135.7 8.3 %flux_stencil.1 = (f32[8,64,750]{2,1,0:T(8,128)}, f32[8,64,750]{2,1,0:T(8,128)}, f32[8,64,750]{2,1,0:T(8,128)}) custom-call(f32[3,8,64,768]{3,2,1,0:T(8,128)} %get-tuple-element.5.filt_ref, f32[3,2,8,1,768]{4,3,2,1,0:T(1,128)} %get-tuple-element.6.edge_ref, f32[8,64,750]{2,1,0:T(8,128)} %tracer_ref.1, f32[64]{0:T(128)} %row_scale_ref.1), custom_call_target="tpu_custom_call" | custom-call | tf_op jit(solution)/shard_map/flux_stencil/pallas_call | solution.py:366

commit v2 on v1

v2 whole, which is shorter than its diff:
```python
import functools
import math

import numpy as np
import jax
import jax.numpy as jnp
from jax import lax
from jax.experimental import pallas as pl
from jax.experimental.pallas import tpu as pltpu
from jax.sharding import PartitionSpec as P

NLON = 12000
SEG = 750
PAD = 768
LANES = 128
MESH = pl.DeviceIdType.MESH
F32 = jnp.float32
BF16 = jnp.bfloat16
ROOT_HALF = math.sqrt(0.5)
courant = 0.5


def phase(steps):
    angle = 2.0 * np.pi * (np.asarray(steps, dtype=np.int64) % NLON) / NLON
    return np.stack([np.cos(angle), np.sin(angle)]).astype(np.float32)


def small_tables():
    k2 = np.arange(128)
    start = (750 * np.arange(2)[:, None] + 32 * np.arange(24)[None, :]).reshape(48)
    inner = np.arange(32)
    last = np.where(inner == 31, -1 - 736, inner)
    coarse, fine = [], []
    for mult in (8 * k2, 8 * k2 + 4):
        coarse.append(phase(start[:, None] * mult[None, :]))
        fine.append(np.stack([phase(b[:, None] * mult[None, :]) for b in (inner, last)]))
    lanes = np.arange(PAD)
    lanes = np.where(lanes == PAD - 1, -1, lanes)
    place = 750 * np.arange(2)[:, None] + lanes[None, :]
    twiddle = np.stack([np.stack([phase(k1 * (1500 * d + place)) for k1 in (1, 2, 3)]) for d in range(8)])
    return np.stack(coarse), np.stack(fine), twiddle[:, :, :, :, None, :]


def split(values):
    high = values.astype(BF16)
    return high, (values - high.astype(F32)).astype(BF16)


def dot3(high, low, table_high, table_low, dims):
    def one(a, b):
        return lax.dot_general(a, b, (dims, ((), ())), preferred_element_type=F32)

    return one(high, table_high) + (one(high, table_low) + one(low, table_high))


def filter_kernel(
    u_ref, v_ref, q_ref, cut_ref, scale_ref, coarse_ref, fine_ref, tw_ref,
    filt_ref, edge_ref,
    raw_u, raw_x, table, y_h, y_l, zed,
    prod_u, peer_u, spec_u, prod_x, part_x, spec_x,
    back_u, back_x, edge_u, edge_x,
    gather_s, gather_r, swap_s, swap_r, part_s, part_r, whole_s, whole_r,
    back_s, back_r, edge_s, edge_r, own,
):
    lat = lax.axis_index("lat")
    me = lax.axis_index("lon")
    half, turn, core = me // 8, (me // 2) % 4, me % 2
    fields = (u_ref, v_ref, q_ref)

    def count(f):
        return 8 if f == 0 else 4

    def mine(f):
        return me % 8 if f == 0 else 2 * half + core

    def lon_of(f, member):
        return 8 * half + member if f == 0 else 8 * (member // 2) + 2 * turn + member % 2

    def block(f, ref, member):
        rows = 64 // count(f)
        return ref.at[:, pl.ds(pl.multiple_of(rows * member, rows), rows)]

    def raw(f, member):
        return raw_u.at[member] if f == 0 else raw_x.at[f - 1, member]

    def back(f, member):
        return back_u.at[member] if f == 0 else back_x.at[f - 1, member]

    def edge_out(f, member):
        return edge_u.at[member] if f == 0 else edge_x.at[f - 1, member]

    def remote(src, dst, send, recv, lon, at=None):
        place = {"lon": lon} if at is None else {"lat": at, "lon": lon}
        return pltpu.make_async_remote_copy(
            src_ref=src, dst_ref=dst, send_sem=send, recv_sem=recv, device_id=place, device_id_type=MESH
        )

    def gather(f, i):
        dest = (mine(f) + i) % count(f)
        return remote(
            block(f, fields[f], dest), raw(f, mine(f)), gather_s.at[f, i], gather_r.at[f, i], lon_of(f, dest)
        )

    def own_gather(f):
        return pltpu.make_async_copy(block(f, fields[f], mine(f)), raw(f, mine(f)), own.at[f])

    def scatter(f, i):
        dest = (mine(f) + i) % count(f)
        return remote(
            back(f, dest), block(f, filt_ref.at[f], mine(f)), back_s.at[f, i], back_r.at[f, i], lon_of(f, dest)
        )

    def own_scatter(f):
        return pltpu.make_async_copy(back(f, mine(f)), block(f, filt_ref.at[f], mine(f)), own.at[3 + f])

    def swap():
        return remote(prod_u, peer_u, swap_s, swap_r, (me + 8) % 16)

    def quarter(ref, y):
        return ref.at[:, pl.ds(pl.multiple_of(32 * y, 32), 32)]

    def part(f, i):
        to = (turn + i) % 4
        return remote(
            quarter(prod_x.at[f - 1], to), part_x.at[f - 1, i - 1],
            part_s.at[f - 1, i], part_r.at[f - 1, i], 8 * half + 2 * to + core,
        )

    def whole(f, i):
        to = (turn + i) % 4
        return remote(
            quarter(spec_x.at[f - 1], turn), quarter(spec_x.at[f - 1], turn),
            whole_s.at[f - 1, i], whole_r.at[f - 1, i], 8 * half + 2 * to + core,
        )

    def edge(f, side, member):
        return remote(
            edge_out(f, member), edge_ref.at[f, side], edge_s.at[f, member], edge_r.at[f, side],
            lon_of(f, member), lat + (1 - 2 * side),
        )

    def sides(f):
        return (
            (0, jnp.logical_and(mine(f) == count(f) - 1, lat < 7), lat > 0),
            (1, jnp.logical_and(mine(f) == 0, lat > 0), lat < 7),
        )

    def each(first, last, action):
        def body(i, carry):
            action(i)
            return carry

        lax.fori_loop(first, last, body, 0)

    barrier = pltpu.get_barrier_semaphore()

    def greet(lon, at):
        pl.semaphore_signal(barrier, inc=1, device_id={"lat": at, "lon": lon}, device_id_type=MESH)

    each(1, 16, lambda i: greet((me + i) % 16, lat))

    @pl.when(lat > 0)
    def _():
        each(0, 16, lambda i: greet(i, lat - 1))

    @pl.when(lat < 7)
    def _():
        each(0, 16, lambda i: greet(i, lat + 1))

    pl.semaphore_wait(barrier, 15 + 16 * jnp.minimum(lat, 1) + 16 * jnp.minimum(7 - lat, 1))

    for f in (1, 0, 2):
        own_gather(f).start()
        each(1, count(f), lambda i, f=f: gather(f, i).start())

    for kind in range(2):
        for c in range(2):
            def fill(a, kind=kind, c=c):
                tail = jnp.where(a == 23, 1, 0)
                c1 = coarse_ref[kind, 0, pl.ds(24 * c + a, 1), :]
                s1 = coarse_ref[kind, 1, pl.ds(24 * c + a, 1), :]
                c2 = fine_ref[kind, tail, 0]
                s2 = fine_ref[kind, tail, 1]
                rows = pl.ds(pl.multiple_of(32 * a, 32), 32)
                for side, value in enumerate((c1 * c2 - s1 * s2, s1 * c2 + c1 * s2)):
                    high, low = split(value)
                    table[kind, c, rows, pl.ds(128 * side, 128)] = high
                    table[kind, c, rows, pl.ds(256 + 128 * side, 128)] = low
                    table[kind, c, rows, pl.ds(512 + 128 * side, 128)] = high

            each(0, 24, fill)
    for r in range(8):
        for c in range(2):
            y_h[c, r, :, 640:] = jnp.zeros((128, 128), BF16)
            y_l[c, r, :, 640:] = jnp.zeros((128, 128), BF16)

    row_at = lax.broadcasted_iota(jnp.int32, (8, 256), 0)
    lane_at = lax.broadcasted_iota(jnp.int32, (8, 256), 1)
    k2 = lane_at % 128
    sign = jnp.where(lane_at < 128, 1.0, -1.0).astype(F32)
    zero = jnp.where(k2 == 0, F32(0.5), F32(1.0))

    def limits_of(first):
        limits = jnp.zeros((8, 256), jnp.int32)
        for row in range(8):
            limits = jnp.where(row_at == row, cut_ref[first + row], limits)
        return limits

    def weights_of(first):
        limits = limits_of(first)

        def kept(k):
            return jnp.where(k < limits, F32(2.0 / NLON), F32(0.0))

        pairs = []
        for k1 in (1, 2, 3):
            above, below = kept(8 * k2 + 4 + k1), kept(8 * k2 + 4 - k1)
            pairs.append((above + below, (above - below) * sign))
        return kept(8 * k2 + 4), kept(8 * k2) * zero, pairs

    def keep(rows, weights):
        centre, single, pairs = weights
        out = [rows[0] * centre]
        for k1 in (1, 2, 3):
            both, odd = pairs[k1 - 1]
            r1, r2 = rows[2 * k1 - 1], rows[2 * k1]
            swap1 = jnp.concatenate([r1[:, 128:], r1[:, :128]], axis=1)
            swap2 = jnp.concatenate([r2[:, 128:], r2[:, :128]], axis=1)
            out += [both * r1 + odd * swap2, both * r2 - odd * swap1]
        return out + [rows[7] * single]

    flip = jnp.where(turn % 2 == 0, F32(1.0), F32(-1.0))

    def analyse(f, target):
        lines = 64 if f == 0 else 128
        base = 4 * half if f == 0 else turn

        def first_stage(step):
            at = pl.ds(pl.multiple_of(16 * step, 16), 16)
            for c in range(2):
                for lo in range(0, SEG, LANES):
                    hi = min(SEG, lo + LANES)
                    if f == 0:
                        x = [raw_u[2 * d + c, pl.ds(2 * step, 2), :, lo:hi].reshape(16, hi - lo) for d in range(4)]
                        s02, s13 = x[0] + x[2], x[1] + x[3]
                        minus, plus = (x[3] - x[1]) * ROOT_HALF, (x[1] + x[3]) * -ROOT_HALF
                        first, final = s02 - s13, s02 + s13
                        parts = (
                            (x[0] + minus, -x[2] - plus),
                            (x[0] - x[2], x[1] - x[3]),
                            (x[0] - minus, x[2] - plus),
                        )
                    else:
                        x0, x1 = raw_x[f - 1, c, step, :, lo:hi], raw_x[f - 1, 2 + c, step, :, lo:hi]
                        final = x0 + x1
                        first, odd = final * flip, (x0 - x1) * flip
                        parts = ((odd, None), (first, None), (odd, None))
                    rows = [first]
                    for k1, (re, im) in enumerate(parts):
                        co, si = tw_ref[base, k1, 0, c, :, lo:hi], tw_ref[base, k1, 1, c, :, lo:hi]
                        if im is None:
                            rows += [re * co, -(re * si)]
                        else:
                            rows += [re * co + im * si, im * co - re * si]
                    rows.append(final)
                    for r, value in enumerate(rows):
                        high, low = split(value)
                        y_h[c, r, at, lo:hi] = high
                        y_l[c, r, at, lo:hi] = low

        each(0, lines // 16, first_stage)
        for kind, r0, r1 in ((1, 0, 7), (0, 7, 8)):
            total = None
            for c in range(2):
                high = y_h[c, r0:r1, 0:lines, :].reshape((r1 - r0) * lines, PAD)
                low = y_l[c, r0:r1, 0:lines, :].reshape((r1 - r0) * lines, PAD)
                value = dot3(
                    high, low, table[kind, c, :, 0:256], table[kind, c, :, 256:512], ((1,), (0,))
                )
                total = value if total is None else total + value
            target[r0:r1] = total.reshape(r1 - r0, lines, 256)

    def synthesise(f, spec):
        lines = 64 if f == 0 else 128
        base = 4 * half if f == 0 else turn
        for kind, r0, r1 in ((1, 0, 7), (0, 7, 8)):
            high, low = split(spec[r0:r1].reshape((r1 - r0) * lines, 256))
            both = jnp.concatenate([high, high, low], axis=1)
            for c in range(2):
                zed[c, r0:r1, 0:lines] = lax.dot_general(
                    both, table[kind, c], (((1,), (1,)), ((), ())), preferred_element_type=F32
                ).reshape(r1 - r0, lines, PAD)

        def last_stage(step):
            at = pl.ds(pl.multiple_of(8 * step, 8), 8)
            for c in range(2):
                for lo in range(0, PAD, LANES):
                    hi = lo + LANES
                    z = [zed[c, r, at, lo:hi] for r in range(8)]
                    tw = [(tw_ref[base, k1, 0, c, :, lo:hi], tw_ref[base, k1, 1, c, :, lo:hi]) for k1 in range(3)]
                    real = [z[2 * k1 + 1] * tw[k1][0] - z[2 * k1 + 2] * tw[k1][1] for k1 in range(3)]
                    if f == 0:
                        (ar, br, cr) = real
                        ai, bi, ci = [z[2 * k1 + 2] * tw[k1][0] + z[2 * k1 + 1] * tw[k1][1] for k1 in range(3)]
                        up, down = z[0] + z[7], z[0] - z[7]
                        p, m = (ar - cr) * ROOT_HALF, (ai + ci) * ROOT_HALF
                        outs = (up + br + (ar + cr), -(down - bi + (p - m)), up - br + (ci - ai), (p + m) - (down + bi))
                        for d in range(4):
                            back_u[2 * d + c, step, :, lo:hi] = outs[d]
                    else:
                        even, odd = (z[0] + real[1]) * flip + z[7], (real[0] + real[2]) * flip
                        rows = pl.ds(pl.multiple_of(8 * (step % 2), 8), 8)
                        back_x[f - 1, c, step // 2, rows, lo:hi] = even + odd
                        back_x[f - 1, 2 + c, step // 2, rows, lo:hi] = even - odd

        each(0, lines // 8, last_stage)
        own_scatter(f).start()

    def send_edges(f):
        for side, sends, _ in sides(f):
            @pl.when(sends)
            def _(side=side):
                row = (64 // count(f) - 1) * (1 - side)
                at = 63 * (1 - side)
                factor = 1.0 / jnp.full((1, PAD), scale_ref[at], F32) if f < 2 else None

                def pack(member):
                    for level in range(8):
                        value = back(f, member)[level, row:row + 1, :]
                        edge_out(f, member)[level] = value if factor is None else value * factor

                each(0, count(f), pack)
                each(0, count(f), lambda member: edge(f, side, member).start())

    def send_back(f):
        each(1, count(f), lambda i: scatter(f, i).start())
        send_edges(f)

    def analyse_x(f):
        own_gather(f).wait()
        each(1, 4, lambda i: gather(f, i).wait_recv())
        analyse(f, prod_x.at[f - 1])
        each(1, 4, lambda i: part(f, i).start())

    def add_x(f):
        each(1, 4, lambda i: part(f, i).wait_recv())
        weights = [weights_of(16 * mine(f) + 8 * g) for g in range(2)]
        for step in range(4):
            at = pl.ds(pl.multiple_of(32 * turn + 8 * step, 8), 8)
            here = pl.ds(8 * step, 8)
            rows = []
            for r in range(8):
                value = prod_x[f - 1, r, at, :] + part_x[f - 1, 1, r, here, :]
                rows.append(value + (part_x[f - 1, 0, r, here, :] + part_x[f - 1, 2, r, here, :]))
            for r, value in enumerate(keep(rows, weights[step % 2])):
                spec_x[f - 1, r, at, :] = value
        each(1, 4, lambda i: whole(f, i).start())

    def synthesise_x(f):
        each(1, 4, lambda i: whole(f, i).wait_recv())
        synthesise(f, spec_x.at[f - 1])

    analyse_x(1)

    own_gather(0).wait()
    each(1, 8, lambda i: gather(0, i).wait_recv())
    analyse(0, prod_u)
    swap().start()

    add_x(1)
    analyse_x(2)
    synthesise_x(1)
    send_back(1)

    swap().wait_recv()
    weights = weights_of(8 * mine(0))

    def add_u(step):
        at = pl.ds(pl.multiple_of(8 * step, 8), 8)
        rows = [prod_u[r, at, :] + peer_u[r, at, :] for r in range(8)]
        for r, value in enumerate(keep(rows, weights)):
            spec_u[r, at, :] = value

    each(0, 8, add_u)
    synthesise(0, spec_u)

    add_x(2)
    send_back(0)
    synthesise_x(2)
    send_back(2)

    swap().wait_send()
    for f in (1, 0, 2):
        own_scatter(f).wait()
        if f > 0:
            each(1, 4, lambda i, f=f: part(f, i).wait_send())
            each(1, 4, lambda i, f=f: whole(f, i).wait_send())

        def finish(i, f=f):
            gather(f, i).wait_send()
            scatter(f, i).wait_send()
            scatter(f, i).wait_recv()

        each(1, count(f), finish)
        for side, sends, gets in sides(f):
            @pl.when(sends)
            def _(f=f, side=side):
                each(0, count(f), lambda member: edge(f, side, member).wait_send())

            @pl.when(gets)
            def _(f=f, side=side):
                remote(
                    edge_out(f, 0), edge_ref.at[f, side], edge_s.at[f, 0], edge_r.at[f, side], (me + 1) % 16
                ).wait_recv()


def stencil_kernel(filt_ref, edge_ref, tracer_ref, row_scale_ref, t_ref, d_ref, z_ref, scale_ref, inv_ref):
    lat = lax.axis_index("lat")

    @pl.when(pl.program_id(0) == 0)
    def _():
        def spread(row, carry):
            scale_ref[pl.ds(row, 1), :] = jnp.full((1, LANES), row_scale_ref[row], F32)
            return carry

        lax.fori_loop(0, 64, spread, 0, unroll=8)
        inv_ref[...] = 1.0 / scale_ref[...]

    scale = jnp.concatenate([scale_ref[...]] * (PAD // LANES), axis=1)
    inv = jnp.concatenate([inv_ref[...]] * (PAD // LANES), axis=1)
    first = lax.broadcasted_iota(jnp.int32, (64, PAD), 0) == 0
    last = lax.broadcasted_iota(jnp.int32, (64, PAD), 0) == 63

    def change(field, values):
        above = jnp.where(lat > 0, edge_ref[field, 0, 0], F32(0.0))
        below = jnp.where(lat < 7, edge_ref[field, 1, 0], F32(0.0))
        north = jnp.where(first, above, pltpu.roll(values, 1, 0))
        south = jnp.where(last, below, pltpu.roll(values, 63, 0))
        return south - north

    def east_west(values):
        return pltpu.roll(values, PAD - 1, 1) - pltpu.roll(values, 1, 1)

    u, v, q = filt_ref[0, 0], filt_ref[1, 0], filt_ref[2, 0]
    d_ref[0] = (scale * (east_west(u) + change(1, v * inv)))[:, :SEG]
    z_ref[0] = (scale * (east_west(v) - change(0, u * inv)))[:, :SEG]
    flux = u * scale * east_west(q) + v * change(2, q)
    t_ref[0] = tracer_ref[0] - courant * flux[:, :SEG]


def on_device(tables, wind_u, wind_v, tracer, cutoff, row_scale):
    coarse, fine, twiddle = (jnp.asarray(t) for t in tables)
    hbm = pl.BlockSpec(memory_space=pl.ANY)
    vmem = pl.BlockSpec(memory_space=pltpu.VMEM)
    smem = pl.BlockSpec(memory_space=pltpu.SMEM)
    dma = pltpu.SemaphoreType.DMA
    filt, edge = pl.pallas_call(
        filter_kernel,
        name="polar_filter",
        out_shape=(
            jax.ShapeDtypeStruct((3, 8, 64, PAD), F32),
            jax.ShapeDtypeStruct((3, 2, 8, 1, PAD), F32),
        ),
        in_specs=[hbm, hbm, hbm, smem, smem, vmem, vmem, vmem],
        out_specs=(hbm, hbm),
        scratch_shapes=[
            pltpu.VMEM((8, 8, 8, SEG), F32),
            pltpu.VMEM((2, 4, 8, 16, SEG), F32),
            pltpu.VMEM((2, 2, PAD, PAD), BF16),
            pltpu.VMEM((2, 8, 128, PAD), BF16),
            pltpu.VMEM((2, 8, 128, PAD), BF16),
            pltpu.VMEM((2, 8, 128, PAD), F32),
            pltpu.VMEM((8, 64, 256), F32),
            pltpu.VMEM((8, 64, 256), F32),
            pltpu.VMEM((8, 64, 256), F32),
            pltpu.VMEM((2, 8, 128, 256), F32),
            pltpu.VMEM((2, 3, 8, 32, 256), F32),
            pltpu.VMEM((2, 8, 128, 256), F32),
            pltpu.VMEM((8, 8, 8, PAD), F32),
            pltpu.VMEM((2, 4, 8, 16, PAD), F32),
            pltpu.VMEM((8, 8, 1, PAD), F32),
            pltpu.VMEM((2, 4, 8, 1, PAD), F32),
            dma((3, 8)), dma((3, 8)), dma, dma, dma((2, 4)), dma((2, 4)), dma((2, 4)), dma((2, 4)),
            dma((3, 8)), dma((3, 8)), dma((3, 8)), dma((3, 2)), dma((6,)),
        ],
        compiler_params=pltpu.CompilerParams(has_side_effects=True, collective_id=0, vmem_limit_bytes=60 * 1024 * 1024),
    )(wind_u, wind_v, tracer, cutoff, row_scale, coarse, fine, twiddle)
    level = pl.BlockSpec((1, 64, SEG), lambda k: (k, 0, 0))
    shape = jax.ShapeDtypeStruct((8, 64, SEG), F32)
    return pl.pallas_call(
        stencil_kernel,
        name="flux_stencil",
        grid=(8,),
        out_shape=(shape, shape, shape),
        in_specs=[
            pl.BlockSpec((3, 1, 64, PAD), lambda k: (0, k, 0, 0)),
            pl.BlockSpec((3, 2, 1, 1, PAD), lambda k: (0, 0, k, 0, 0)),
            level, smem,
        ],
        out_specs=(level, level, level),
        scratch_shapes=[pltpu.VMEM((64, LANES), F32), pltpu.VMEM((64, LANES), F32)],
    )(filt, edge, tracer, row_scale)


def solution(mesh):
    in_specs = (
        P(None, "lat", "lon"),
        P(None, "lat", "lon"),
        P(None, "lat", "lon"),
        P("lat"),
        P("lat"),
    )
    out_specs = (P(None, "lat", "lon"), P(None, "lat", "lon"), P(None, "lat", "lon"))
    return jax.shard_map(
        functools.partial(on_device, small_tables()),
        mesh=mesh, in_specs=in_specs, out_specs=out_specs, check_vma=False,
    )
```

time: 144 us -> 112 us (0.78)
  the two profiles are of different devices: /device:TPU:19 before, /device:TPU:57 now
where the time goes in v2:
time: 112 us
  Pallas kernels  111 us (99%)
    pallas_call x1, Pallas kernels, on_device(): pl.pallas_call(filter_kernel, name='polar_filter', out_shape=(jax.ShapeDt...  103 us
    pallas_call x1, Pallas kernels, on_device(): pl.pallas_call(stencil_kernel, name='flux_stencil', grid=(8,), out_shape=...  8.32 us

profile of v2, /device:TPU:57, one launch (start us, length us, event | category | flops | bytes accessed | tf_op | source)
XLA Modules:
  0.0 111.9 jit_solution(12382053552670743694)
XLA Ops:
  0.6 102.9 %polar_filter.1 = (f32[3,8,64,768]{3,2,1,0:T(8,128)}, f32[3,2,8,1,768]{4,3,2,1,0:T(1,128)}) custom-call(f32[8,64,750]{2,1,0:T(8,128)} %u_ref.1, f32[8,64,750]{2,1,0:T(8,128)} %v_ref.1, f32[8,64,750]{2,1,0:T(8,128)} %tracer_ref.1, s32[64]{0:T(128)} %cut_ref.1, f32[64]{0:T(128)} %row_scale_ref.1, f32[2,2,48,128]{3,2,1,0:T(8,128)} %constant.6.clone.coarse_ref, ...), custom_call_target="tpu_custom_call" | custom-call | tf_op jit(solution)/shard_map/polar_filter/pallas_call | solution.py:457
  103.5 8.3 %flux_stencil.1 = (f32[8,64,750]{2,1,0:T(8,128)}, f32[8,64,750]{2,1,0:T(8,128)}, f32[8,64,750]{2,1,0:T(8,128)}) custom-call(f32[3,8,64,768]{3,2,1,0:T(8,128)} %get-tuple-element.5.filt_ref, f32[3,2,8,1,768]{4,3,2,1,0:T(1,128)} %get-tuple-element.6.edge_ref, f32[8,64,750]{2,1,0:T(8,128)} %tracer_ref.1, f32[64]{0:T(128)} %row_scale_ref.1), custom_call_target="tpu_custom_call" | custom-call | tf_op jit(solution)/shard_map/flux_stencil/pallas_call | solution.py:490

commit v3 on v2

--- a/solution.py
+++ b/solution.py
@@ -18,6 +18,7 @@
 BF16 = jnp.bfloat16
 ROOT_HALF = math.sqrt(0.5)
 courant = 0.5
+STREAMS = ((0, 0, 8, True, 0), (1, 0, 8, False, 0), (2, 0, 6, False, 0), (2, 6, 2, True, 8))
 
 
 def phase(steps):
@@ -57,7 +58,7 @@
     u_ref, v_ref, q_ref, cut_ref, scale_ref, coarse_ref, fine_ref, tw_ref,
     filt_ref, edge_ref,
     raw_u, raw_x, table, y_h, y_l, zed,
-    prod_u, peer_u, spec_u, prod_x, part_x, spec_x,
+    prod_u, peer_u, spec_u, prod_x, part_x, relay_x, spec_x,
     back_u, back_x, edge_u, edge_x,
     gather_s, gather_r, swap_s, swap_r, part_s, part_r, whole_s, whole_r,
     back_s, back_r, edge_s, edge_r, own,
@@ -67,27 +68,42 @@
     half, turn, core = me // 8, (me // 2) % 4, me % 2
     fields = (u_ref, v_ref, q_ref)
 
+    def column(f):
+        return STREAMS[f][3]
+
     def count(f):
-        return 8 if f == 0 else 4
+        return 8 if column(f) else 4
 
     def mine(f):
-        return me % 8 if f == 0 else 2 * half + core
+        return me % 8 if column(f) else 2 * half + core
 
     def lon_of(f, member):
-        return 8 * half + member if f == 0 else 8 * (member // 2) + 2 * turn + member % 2
+        return 8 * half + member if column(f) else 8 * (member // 2) + 2 * turn + member % 2
+
+    def levels(f):
+        return pl.ds(STREAMS[f][1], STREAMS[f][2])
+
+    def place(f):
+        return pl.ds(STREAMS[f][4], STREAMS[f][2])
 
     def block(f, ref, member):
         rows = 64 // count(f)
-        return ref.at[:, pl.ds(pl.multiple_of(rows * member, rows), rows)]
+        return ref.at[levels(f), pl.ds(pl.multiple_of(rows * member, rows), rows)]
+
+    def source(f):
+        return fields[STREAMS[f][0]]
+
+    def result(f):
+        return filt_ref.at[STREAMS[f][0]]
 
     def raw(f, member):
-        return raw_u.at[member] if f == 0 else raw_x.at[f - 1, member]
+        return raw_u.at[member, place(f)] if column(f) else raw_x.at[f - 1, member, place(f)]
 
     def back(f, member):
-        return back_u.at[member] if f == 0 else back_x.at[f - 1, member]
+        return back_u.at[member, place(f)] if column(f) else back_x.at[f - 1, member, place(f)]
 
     def edge_out(f, member):
-        return edge_u.at[member] if f == 0 else edge_x.at[f - 1, member]
+        return edge_u.at[member, place(f)] if column(f) else edge_x.at[f - 1, member, place(f)]
 
     def remote(src, dst, send, recv, lon, at=None):
         place = {"lon": lon} if at is None else {"lat": at, "lon": lon}
@@ -98,44 +114,67 @@
     def gather(f, i):
         dest = (mine(f) + i) % count(f)
         return remote(
-            block(f, fields[f], dest), raw(f, mine(f)), gather_s.at[f, i], gather_r.at[f, i], lon_of(f, dest)
+            block(f, source(f), dest), raw(f, mine(f)), gather_s.at[f, i], gather_r.at[f, i], lon_of(f, dest)
         )
 
     def own_gather(f):
-        return pltpu.make_async_copy(block(f, fields[f], mine(f)), raw(f, mine(f)), own.at[f])
+        return pltpu.make_async_copy(block(f, source(f), mine(f)), raw(f, mine(f)), own.at[f])
 
     def scatter(f, i):
         dest = (mine(f) + i) % count(f)
         return remote(
-            back(f, dest), block(f, filt_ref.at[f], mine(f)), back_s.at[f, i], back_r.at[f, i], lon_of(f, dest)
+            back(f, dest), block(f, result(f), mine(f)), back_s.at[f, i], back_r.at[f, i], lon_of(f, dest)
         )
 
     def own_scatter(f):
-        return pltpu.make_async_copy(back(f, mine(f)), block(f, filt_ref.at[f], mine(f)), own.at[3 + f])
+        return pltpu.make_async_copy(back(f, mine(f)), block(f, result(f), mine(f)), own.at[4 + f])
 
     def swap():
         return remote(prod_u, peer_u, swap_s, swap_r, (me + 8) % 16)
 
-    def quarter(ref, y):
-        return ref.at[:, pl.ds(pl.multiple_of(32 * y, 32), 32)]
-
-    def part(f, i):
-        to = (turn + i) % 4
+    odd_turn = turn % 2
+    near = (turn + 1 - 2 * odd_turn, (turn + 3 + 2 * odd_turn) % 4)
+    opposite = (turn + 2) % 4
+
+    def size(f):
+        return 4 * STREAMS[f][2]
+
+    def quarter(f, ref, y, rows):
+        return ref.at[f - 1, rows, pl.ds(pl.multiple_of(size(f) * y, 8), size(f))]
+
+    def four(d):
+        return pl.ds(4 * d, 4)
+
+    def beside(d):
+        return 8 * half + 2 * near[d] + core
+
+    def part(f, d, slot):
+        if slot == 2:
+            src = relay_x.at[f - 1, d, :, pl.ds(0, size(f))]
+        else:
+            src = quarter(f, prod_x, near[d] if slot == 0 else opposite, four(d))
         return remote(
-            quarter(prod_x.at[f - 1], to), part_x.at[f - 1, i - 1],
-            part_s.at[f - 1, i], part_r.at[f - 1, i], 8 * half + 2 * to + core,
+            src, part_x.at[f - 1, d, slot, :, pl.ds(0, size(f))],
+            part_s.at[f - 1, d, slot], part_r.at[f - 1, d, slot], beside(d),
         )
 
-    def whole(f, i):
-        to = (turn + i) % 4
-        return remote(
-            quarter(spec_x.at[f - 1], turn), quarter(spec_x.at[f - 1], turn),
-            whole_s.at[f - 1, i], whole_r.at[f - 1, i], 8 * half + 2 * to + core,
-        )
+    def whole(f, d, slot):
+        if slot == 0:
+            piece = quarter(f, spec_x, turn, pl.ds(0, 8))
+        else:
+            piece = quarter(f, spec_x, near[1 - d], four(d))
+        return remote(piece, piece, whole_s.at[f - 1, d, slot], whole_r.at[f - 1, d, slot], beside(d))
+
+    def whole_arrival(f, d, slot):
+        if slot == 0:
+            piece = quarter(f, spec_x, near[d], pl.ds(0, 8))
+        else:
+            piece = quarter(f, spec_x, opposite, four(d))
+        return remote(piece, piece, whole_s.at[f - 1, d, slot], whole_r.at[f - 1, d, slot], beside(d))
 
     def edge(f, side, member):
         return remote(
-            edge_out(f, member), edge_ref.at[f, side], edge_s.at[f, member], edge_r.at[f, side],
+            edge_out(f, member), edge_ref.at[STREAMS[f][0], side, levels(f)], edge_s.at[f, member], edge_r.at[f, side],
             lon_of(f, member), lat + (1 - 2 * side),
         )
 
@@ -157,19 +196,28 @@
     def greet(lon, at):
         pl.semaphore_signal(barrier, inc=1, device_id={"lat": at, "lon": lon}, device_id_type=MESH)
 
-    each(1, 16, lambda i: greet((me + i) % 16, lat))
+    each(1, 8, lambda i: greet(8 * half + (me + i) % 8, lat))
+    for other in (core, 1 - core):
+        greet(8 * (1 - half) + 2 * turn + other, lat)
 
     @pl.when(lat > 0)
     def _():
-        each(0, 16, lambda i: greet(i, lat - 1))
+        greet(8 * half + 7, lat - 1)
+        greet(2 * turn + 9, lat - 1)
 
     @pl.when(lat < 7)
     def _():
-        each(0, 16, lambda i: greet(i, lat + 1))
-
-    pl.semaphore_wait(barrier, 15 + 16 * jnp.minimum(lat, 1) + 16 * jnp.minimum(7 - lat, 1))
-
-    for f in (1, 0, 2):
+        greet(8 * half, lat + 1)
+        greet(2 * turn, lat + 1)
+
+    def either(yes):
+        return jnp.where(yes, 1, 0)
+
+    lower = 8 * either(me % 8 == 7) + 4 * either(half + core == 2)
+    upper = 8 * either(me % 8 == 0) + 4 * either(half + core == 0)
+    pl.semaphore_wait(barrier, 9 + lower * either(lat < 7) + upper * either(lat > 0))
+
+    for f in (1, 0, 3, 2):
         own_gather(f).start()
         each(1, count(f), lambda i, f=f: gather(f, i).start())
 
@@ -232,15 +280,15 @@
     flip = jnp.where(turn % 2 == 0, F32(1.0), F32(-1.0))
 
     def analyse(f, target):
-        lines = 64 if f == 0 else 128
-        base = 4 * half if f == 0 else turn
+        lines = 80 if column(f) else 16 * STREAMS[f][2]
+        base = 4 * half if column(f) else turn
 
         def first_stage(step):
             at = pl.ds(pl.multiple_of(16 * step, 16), 16)
             for c in range(2):
                 for lo in range(0, SEG, LANES):
                     hi = min(SEG, lo + LANES)
-                    if f == 0:
+                    if column(f):
                         x = [raw_u[2 * d + c, pl.ds(2 * step, 2), :, lo:hi].reshape(16, hi - lo) for d in range(4)]
                         s02, s13 = x[0] + x[2], x[1] + x[3]
                         minus, plus = (x[3] - x[1]) * ROOT_HALF, (x[1] + x[3]) * -ROOT_HALF
@@ -278,13 +326,13 @@
                     high, low, table[kind, c, :, 0:256], table[kind, c, :, 256:512], ((1,), (0,))
                 )
                 total = value if total is None else total + value
-            target[r0:r1] = total.reshape(r1 - r0, lines, 256)
+            target[r0:r1, 0:lines] = total.reshape(r1 - r0, lines, 256)
 
     def synthesise(f, spec):
-        lines = 64 if f == 0 else 128
-        base = 4 * half if f == 0 else turn
+        lines = 80 if column(f) else 16 * STREAMS[f][2]
+        base = 4 * half if column(f) else turn
         for kind, r0, r1 in ((1, 0, 7), (0, 7, 8)):
-            high, low = split(spec[r0:r1].reshape((r1 - r0) * lines, 256))
+            high, low = split(spec[r0:r1, 0:lines].reshape((r1 - r0) * lines, 256))
             both = jnp.concatenate([high, high, low], axis=1)
             for c in range(2):
                 zed[c, r0:r1, 0:lines] = lax.dot_general(
@@ -299,7 +347,7 @@
                     z = [zed[c, r, at, lo:hi] for r in range(8)]
                     tw = [(tw_ref[base, k1, 0, c, :, lo:hi], tw_ref[base, k1, 1, c, :, lo:hi]) for k1 in range(3)]
                     real = [z[2 * k1 + 1] * tw[k1][0] - z[2 * k1 + 2] * tw[k1][1] for k1 in range(3)]
-                    if f == 0:
+                    if column(f):
                         (ar, br, cr) = real
                         ai, bi, ci = [z[2 * k1 + 2] * tw[k1][0] + z[2 * k1 + 1] * tw[k1][1] for k1 in range(3)]
                         up, down = z[0] + z[7], z[0] - z[7]
@@ -314,7 +362,6 @@
                         back_x[f - 1, 2 + c, step // 2, rows, lo:hi] = even - odd
 
         each(0, lines // 8, last_stage)
-        own_scatter(f).start()
 
     def send_edges(f):
         for side, sends, _ in sides(f):
@@ -322,10 +369,10 @@
             def _(side=side):
                 row = (64 // count(f) - 1) * (1 - side)
                 at = 63 * (1 - side)
-                factor = 1.0 / jnp.full((1, PAD), scale_ref[at], F32) if f < 2 else None
+                factor = 1.0 / jnp.full((1, PAD), scale_ref[at], F32) if STREAMS[f][0] < 2 else None
 
                 def pack(member):
-                    for level in range(8):
+                    for level in range(STREAMS[f][2]):
                         value = back(f, member)[level, row:row + 1, :]
                         edge_out(f, member)[level] = value if factor is None else value * factor
 
@@ -333,44 +380,73 @@
                 each(0, count(f), lambda member: edge(f, side, member).start())
 
     def send_back(f):
+        own_scatter(f).start()
         each(1, count(f), lambda i: scatter(f, i).start())
         send_edges(f)
 
+    def arrive(f):
+        own_gather(f).wait()
+        each(1, count(f), lambda i: gather(f, i).wait_recv())
+
     def analyse_x(f):
-        own_gather(f).wait()
-        each(1, 4, lambda i: gather(f, i).wait_recv())
+        arrive(f)
         analyse(f, prod_x.at[f - 1])
-        each(1, 4, lambda i: part(f, i).start())
+        for slot in (1, 0):
+            for d in range(2):
+                part(f, d, slot).start()
+
+    def relay(f):
+        for d in range(2):
+            part(f, 1 - d, 1).wait_recv()
+            at = pl.ds(pl.multiple_of(size(f) * near[d], 8), size(f))
+            relay_x[f - 1, d, :, 0:size(f), :] = (
+                prod_x[f - 1, 4 - 4 * d:8 - 4 * d, at, :] + part_x[f - 1, 1 - d, 1, :, 0:size(f), :]
+            )
+            part(f, d, 2).start()
 
     def add_x(f):
-        each(1, 4, lambda i: part(f, i).wait_recv())
-        weights = [weights_of(16 * mine(f) + 8 * g) for g in range(2)]
-        for step in range(4):
-            at = pl.ds(pl.multiple_of(32 * turn + 8 * step, 8), 8)
+        for d in range(2):
+            part(f, d, 0).wait_recv()
+            part(f, d, 2).wait_recv()
+        groups = size(f) // 8
+        weights = [weights_of(16 * mine(f) + 8 * ((groups * turn + g) % 2)) for g in range(2)]
+        for step in range(groups):
+            at = pl.ds(pl.multiple_of(size(f) * turn + 8 * step, 8), 8)
             here = pl.ds(8 * step, 8)
             rows = []
             for r in range(8):
-                value = prod_x[f - 1, r, at, :] + part_x[f - 1, 1, r, here, :]
-                rows.append(value + (part_x[f - 1, 0, r, here, :] + part_x[f - 1, 2, r, here, :]))
+                d = r // 4
+                value = prod_x[f - 1, r, at, :] + part_x[f - 1, d, 0, r % 4, here, :]
+                rows.append(value + part_x[f - 1, 1 - d, 2, r % 4, here, :])
             for r, value in enumerate(keep(rows, weights[step % 2])):
                 spec_x[f - 1, r, at, :] = value
-        each(1, 4, lambda i: whole(f, i).start())
+        for d in range(2):
+            whole(f, d, 0).start()
+
+    def spread(f):
+        for d in range(2):
+            whole_arrival(f, d, 0).wait_recv()
+        for d in range(2):
+            whole(f, d, 1).start()
 
     def synthesise_x(f):
-        each(1, 4, lambda i: whole(f, i).wait_recv())
+        for d in range(2):
+            whole_arrival(f, d, 1).wait_recv()
         synthesise(f, spec_x.at[f - 1])
 
     analyse_x(1)
-
-    own_gather(0).wait()
-    each(1, 8, lambda i: gather(0, i).wait_recv())
+    arrive(0)
+    arrive(3)
     analyse(0, prod_u)
     swap().start()
-
+    relay(1)
     add_x(1)
     analyse_x(2)
+    spread(1)
+    relay(2)
     synthesise_x(1)
     send_back(1)
+    add_x(2)
 
     swap().wait_recv()
     weights = weights_of(8 * mine(0))
@@ -381,20 +457,23 @@
         for r, value in enumerate(keep(rows, weights)):
             spec_u[r, at, :] = value
 
-    each(0, 8, add_u)
+    each(0, 10, add_u)
+    spread(2)
     synthesise(0, spec_u)
-
-    add_x(2)
     send_back(0)
+    send_back(3)
     synthesise_x(2)
     send_back(2)
 
     swap().wait_send()
-    for f in (1, 0, 2):
+    for f in (1, 0, 3, 2):
         own_scatter(f).wait()
-        if f > 0:
-            each(1, 4, lambda i, f=f: part(f, i).wait_send())
-            each(1, 4, lambda i, f=f: whole(f, i).wait_send())
+        if not column(f):
+            for d in range(2):
+                for slot in range(3):
+                    part(f, d, slot).wait_send()
+                for slot in range(2):
+                    whole(f, d, slot).wait_send()
 
         def finish(i, f=f):
             gather(f, i).wait_send()
@@ -410,7 +489,8 @@
             @pl.when(gets)
             def _(f=f, side=side):
                 remote(
-                    edge_out(f, 0), edge_ref.at[f, side], edge_s.at[f, 0], edge_r.at[f, side], (me + 1) % 16
+                    edge_out(f, 0), edge_ref.at[STREAMS[f][0], side, levels(f)],
+                    edge_s.at[f, 0], edge_r.at[f, side], (me + 1) % 16,
                 ).wait_recv()
 
 
@@ -426,26 +506,36 @@
         lax.fori_loop(0, 64, spread, 0, unroll=8)
         inv_ref[...] = 1.0 / scale_ref[...]
 
-    scale = jnp.concatenate([scale_ref[...]] * (PAD // LANES), axis=1)
-    inv = jnp.concatenate([inv_ref[...]] * (PAD // LANES), axis=1)
-    first = lax.broadcasted_iota(jnp.int32, (64, PAD), 0) == 0
-    last = lax.broadcasted_iota(jnp.int32, (64, PAD), 0) == 63
-
-    def change(field, values):
-        above = jnp.where(lat > 0, edge_ref[field, 0, 0], F32(0.0))
-        below = jnp.where(lat < 7, edge_ref[field, 1, 0], F32(0.0))
-        north = jnp.where(first, above, pltpu.roll(values, 1, 0))
-        south = jnp.where(last, below, pltpu.roll(values, 63, 0))
-        return south - north
-
-    def east_west(values):
-        return pltpu.roll(values, PAD - 1, 1) - pltpu.roll(values, 1, 1)
-
-    u, v, q = filt_ref[0, 0], filt_ref[1, 0], filt_ref[2, 0]
-    d_ref[0] = (scale * (east_west(u) + change(1, v * inv)))[:, :SEG]
-    z_ref[0] = (scale * (east_west(v) - change(0, u * inv)))[:, :SEG]
-    flux = u * scale * east_west(q) + v * change(2, q)
-    t_ref[0] = tracer_ref[0] - courant * flux[:, :SEG]
+    first = lax.broadcasted_iota(jnp.int32, (64, LANES), 0) == 0
+    last = lax.broadcasted_iota(jnp.int32, (64, LANES), 0) == 63
+    lane = lax.broadcasted_iota(jnp.int32, (64, LANES), 1)
+
+    def one_level(level, carry):
+        for lo in range(0, PAD, LANES):
+            hi, width = lo + LANES, min(LANES, SEG - lo)
+            east, west = hi % PAD, (lo - LANES) % PAD
+
+            def change(field, values):
+                above = jnp.where(lat > 0, edge_ref[field, 0, level, :, lo:hi], F32(0.0))
+                below = jnp.where(lat < 7, edge_ref[field, 1, level, :, lo:hi], F32(0.0))
+                north = jnp.where(first, above, pltpu.roll(values, 1, 0))
+                south = jnp.where(last, below, pltpu.roll(values, 63, 0))
+                return south - north
+
+            def east_west(field, values):
+                right = jnp.where(lane == 0, filt_ref[field, level, :, east:east + LANES], values)
+                left = jnp.where(lane == LANES - 1, filt_ref[field, level, :, west:west + LANES], values)
+                return pltpu.roll(right, LANES - 1, 1) - pltpu.roll(left, 1, 1)
+
+            u, v, q = (filt_ref[field, level, :, lo:hi] for field in range(3))
+            scale, inv = scale_ref[...], inv_ref[...]
+            d_ref[level, :, lo:lo + width] = (scale * (east_west(0, u) + change(1, v * inv)))[:, :width]
+            z_ref[level, :, lo:lo + width] = (scale * (east_west(1, v) - change(0, u * inv)))[:, :width]
+            flux = u * scale * east_west(2, q) + v * change(2, q)
+            t_ref[level, :, lo:lo + width] = tracer_ref[level, :, lo:lo + width] - courant * flux[:, :width]
+        return carry
+
+    lax.fori_loop(0, 4, one_level, 0)
 
 
 def on_device(tables, wind_u, wind_v, tracer, cutoff, row_scale):
@@ -464,37 +554,38 @@
         in_specs=[hbm, hbm, hbm, smem, smem, vmem, vmem, vmem],
         out_specs=(hbm, hbm),
         scratch_shapes=[
-            pltpu.VMEM((8, 8, 8, SEG), F32),
+            pltpu.VMEM((8, 10, 8, SEG), F32),
             pltpu.VMEM((2, 4, 8, 16, SEG), F32),
             pltpu.VMEM((2, 2, PAD, PAD), BF16),
             pltpu.VMEM((2, 8, 128, PAD), BF16),
             pltpu.VMEM((2, 8, 128, PAD), BF16),
             pltpu.VMEM((2, 8, 128, PAD), F32),
-            pltpu.VMEM((8, 64, 256), F32),
-            pltpu.VMEM((8, 64, 256), F32),
-            pltpu.VMEM((8, 64, 256), F32),
+            pltpu.VMEM((8, 80, 256), F32),
+            pltpu.VMEM((8, 80, 256), F32),
+            pltpu.VMEM((8, 80, 256), F32),
             pltpu.VMEM((2, 8, 128, 256), F32),
-            pltpu.VMEM((2, 3, 8, 32, 256), F32),
+            pltpu.VMEM((2, 2, 3, 4, 32, 256), F32),
+            pltpu.VMEM((2, 2, 4, 32, 256), F32),
             pltpu.VMEM((2, 8, 128, 256), F32),
-            pltpu.VMEM((8, 8, 8, PAD), F32),
+            pltpu.VMEM((8, 10, 8, PAD), F32),
             pltpu.VMEM((2, 4, 8, 16, PAD), F32),
-            pltpu.VMEM((8, 8, 1, PAD), F32),
+            pltpu.VMEM((8, 10, 1, PAD), F32),
             pltpu.VMEM((2, 4, 8, 1, PAD), F32),
-            dma((3, 8)), dma((3, 8)), dma, dma, dma((2, 4)), dma((2, 4)), dma((2, 4)), dma((2, 4)),
-            dma((3, 8)), dma((3, 8)), dma((3, 8)), dma((3, 2)), dma((6,)),
+            dma((4, 8)), dma((4, 8)), dma, dma, dma((2, 2, 3)), dma((2, 2, 3)), dma((2, 2, 2)), dma((2, 2, 2)),
+            dma((4, 8)), dma((4, 8)), dma((4, 8)), dma((4, 2)), dma((8,)),
         ],
         compiler_params=pltpu.CompilerParams(has_side_effects=True, collective_id=0, vmem_limit_bytes=60 * 1024 * 1024),
     )(wind_u, wind_v, tracer, cutoff, row_scale, coarse, fine, twiddle)
-    level = pl.BlockSpec((1, 64, SEG), lambda k: (k, 0, 0))
+    level = pl.BlockSpec((4, 64, SEG), lambda k: (k, 0, 0))
     shape = jax.ShapeDtypeStruct((8, 64, SEG), F32)
     return pl.pallas_call(
         stencil_kernel,
         name="flux_stencil",
-        grid=(8,),
+        grid=(2,),
         out_shape=(shape, shape, shape),
         in_specs=[
-            pl.BlockSpec((3, 1, 64, PAD), lambda k: (0, k, 0, 0)),
-            pl.BlockSpec((3, 2, 1, 1, PAD), lambda k: (0, 0, k, 0, 0)),
+            pl.BlockSpec((3, 4, 64, PAD), lambda k: (0, k, 0, 0)),
+            pl.BlockSpec((3, 2, 4, 1, PAD), lambda k: (0, 0, k, 0, 0)),
             level, smem,
         ],
         out_specs=(level, level, level),

time: 112 us -> 104 us (0.929)
  the two profiles are of different devices: /device:TPU:57 before, /device:TPU:31 now
where the time goes in v3:
time: 104 us
  Pallas kernels  103 us (99%)
    pallas_call x1, Pallas kernels, on_device(): pl.pallas_call(filter_kernel, name='polar_filter', out_shape=(jax.ShapeDt...  96.6 us
    pallas_call x1, Pallas kernels, on_device(): pl.pallas_call(stencil_kernel, name='flux_stencil', grid=(2,), out_shape=...  6.5 us

profile of v3, /device:TPU:31, one launch (start us, length us, event | category | flops | bytes accessed | tf_op | source)
XLA Modules:
  0.0 103.8 jit_solution(6706002973663074461)
XLA Ops:
  0.6 96.6 %polar_filter.1 = (f32[3,8,64,768]{3,2,1,0:T(8,128)}, f32[3,2,8,1,768]{4,3,2,1,0:T(1,128)}) custom-call(f32[8,64,750]{2,1,0:T(8,128)} %u_ref.1, f32[8,64,750]{2,1,0:T(8,128)} %v_ref.1, f32[8,64,750]{2,1,0:T(8,128)} %tracer_ref.1, s32[64]{0:T(128)} %cut_ref.1, f32[64]{0:T(128)} %row_scale_ref.1, f32[2,2,48,128]{3,2,1,0:T(8,128)} %constant.6.clone.coarse_ref, ...), custom_call_target="tpu_custom_call" | custom-call | tf_op jit(solution)/shard_map/polar_filter/pallas_call | solution.py:547
  97.3 6.5 %flux_stencil.1 = (f32[8,64,750]{2,1,0:T(8,128)}, f32[8,64,750]{2,1,0:T(8,128)}, f32[8,64,750]{2,1,0:T(8,128)}) custom-call(f32[3,8,64,768]{3,2,1,0:T(8,128)} %get-tuple-element.5.filt_ref, f32[3,2,8,1,768]{4,3,2,1,0:T(1,128)} %get-tuple-element.6.edge_ref, f32[8,64,750]{2,1,0:T(8,128)} %tracer_ref.1, f32[64]{0:T(128)} %row_scale_ref.1), custom_call_target="tpu_custom_call" | custom-call | tf_op jit(solution)/shard_map/flux_stencil/pallas_call | solution.py:581

commit v4 on v3

--- a/solution.py
+++ b/solution.py
@@ -55,11 +55,12 @@
 
 
 def filter_kernel(
-    u_ref, v_ref, q_ref, cut_ref, scale_ref, coarse_ref, fine_ref, tw_ref,
+    u_ref, v_ref, q_ref, cut_ref, scale_ref, coarse_far, fine_far, tw_far,
     filt_ref, edge_ref,
     raw_u, raw_x, table, y_h, y_l, zed,
     prod_u, peer_u, spec_u, prod_x, part_x, relay_x, spec_x,
     back_u, back_x, edge_u, edge_x,
+    coarse_ref, fine_ref, tw_ref, seed_s,
     gather_s, gather_r, swap_s, swap_r, part_s, part_r, whole_s, whole_r,
     back_s, back_r, edge_s, edge_r, own,
 ):
@@ -220,6 +221,17 @@
     for f in (1, 0, 3, 2):
         own_gather(f).start()
         each(1, count(f), lambda i, f=f: gather(f, i).start())
+
+    seeds = (
+        pltpu.make_async_copy(coarse_far, coarse_ref, seed_s.at[0]),
+        pltpu.make_async_copy(fine_far, fine_ref, seed_s.at[1]),
+        pltpu.make_async_copy(tw_far.at[turn], tw_ref.at[0], seed_s.at[2]),
+        pltpu.make_async_copy(tw_far.at[4 * half], tw_ref.at[1], seed_s.at[3]),
+    )
+    for seed in seeds:
+        seed.start()
+    for seed in seeds:
+        seed.wait()
 
     for kind in range(2):
         for c in range(2):
@@ -281,7 +293,7 @@
 
     def analyse(f, target):
         lines = 80 if column(f) else 16 * STREAMS[f][2]
-        base = 4 * half if column(f) else turn
+        base = 1 if column(f) else 0
 
         def first_stage(step):
             at = pl.ds(pl.multiple_of(16 * step, 16), 16)
@@ -330,7 +342,7 @@
 
     def synthesise(f, spec):
         lines = 80 if column(f) else 16 * STREAMS[f][2]
-        base = 4 * half if column(f) else turn
+        base = 1 if column(f) else 0
         for kind, r0, r1 in ((1, 0, 7), (0, 7, 8)):
             high, low = split(spec[r0:r1, 0:lines].reshape((r1 - r0) * lines, 256))
             both = jnp.concatenate([high, high, low], axis=1)
@@ -494,23 +506,49 @@
                 ).wait_recv()
 
 
-def stencil_kernel(filt_ref, edge_ref, tracer_ref, row_scale_ref, t_ref, d_ref, z_ref, scale_ref, inv_ref):
+def stencil_kernel(
+    filt_far, edge_far, tracer_far, row_scale_ref, t_far, d_far, z_far,
+    filt_ref, edge_ref, tracer_ref, t_ref, d_ref, z_ref, scale_ref, inv_ref, sems, edge_sem,
+):
     lat = lax.axis_index("lat")
 
-    @pl.when(pl.program_id(0) == 0)
-    def _():
-        def spread(row, carry):
-            scale_ref[pl.ds(row, 1), :] = jnp.full((1, LANES), row_scale_ref[row], F32)
-            return carry
-
-        lax.fori_loop(0, 64, spread, 0, unroll=8)
-        inv_ref[...] = 1.0 / scale_ref[...]
-
+    def arrivals(level):
+        return (
+            pltpu.make_async_copy(filt_far.at[:, level], filt_ref.at[:, level], sems.at[level, 0]),
+            pltpu.make_async_copy(tracer_far.at[level], tracer_ref.at[level], sems.at[level, 1]),
+        )
+
+    def results(level):
+        pairs = ((d_ref, d_far), (z_ref, z_far), (t_ref, t_far))
+        return tuple(
+            pltpu.make_async_copy(near.at[level], far.at[level], sems.at[level, 2 + k])
+            for k, (near, far) in enumerate(pairs)
+        )
+
+    def fetch(level, carry):
+        for copy in arrivals(level):
+            copy.start()
+        return carry
+
+    edges = pltpu.make_async_copy(edge_far, edge_ref, edge_sem)
+    lax.fori_loop(0, 1, fetch, 0)
+    edges.start()
+    lax.fori_loop(1, 8, fetch, 0)
+
+    def spread(row, carry):
+        scale_ref[pl.ds(row, 1), :] = jnp.full((1, LANES), row_scale_ref[row], F32)
+        return carry
+
+    lax.fori_loop(0, 64, spread, 0, unroll=8)
+    inv_ref[...] = 1.0 / scale_ref[...]
+    edges.wait()
     first = lax.broadcasted_iota(jnp.int32, (64, LANES), 0) == 0
     last = lax.broadcasted_iota(jnp.int32, (64, LANES), 0) == 63
     lane = lax.broadcasted_iota(jnp.int32, (64, LANES), 1)
 
     def one_level(level, carry):
+        for copy in arrivals(level):
+            copy.wait()
         for lo in range(0, PAD, LANES):
             hi, width = lo + LANES, min(LANES, SEG - lo)
             east, west = hi % PAD, (lo - LANES) % PAD
@@ -533,15 +571,22 @@
             z_ref[level, :, lo:lo + width] = (scale * (east_west(1, v) - change(0, u * inv)))[:, :width]
             flux = u * scale * east_west(2, q) + v * change(2, q)
             t_ref[level, :, lo:lo + width] = tracer_ref[level, :, lo:lo + width] - courant * flux[:, :width]
+        for copy in results(level):
+            copy.start()
         return carry
 
-    lax.fori_loop(0, 4, one_level, 0)
+    def finish(level, carry):
+        for copy in results(level):
+            copy.wait()
+        return carry
+
+    lax.fori_loop(0, 8, one_level, 0)
+    lax.fori_loop(0, 8, finish, 0)
 
 
 def on_device(tables, wind_u, wind_v, tracer, cutoff, row_scale):
     coarse, fine, twiddle = (jnp.asarray(t) for t in tables)
     hbm = pl.BlockSpec(memory_space=pl.ANY)
-    vmem = pl.BlockSpec(memory_space=pltpu.VMEM)
     smem = pl.BlockSpec(memory_space=pltpu.SMEM)
     dma = pltpu.SemaphoreType.DMA
     filt, edge = pl.pallas_call(
@@ -551,7 +596,7 @@
             jax.ShapeDtypeStruct((3, 8, 64, PAD), F32),
             jax.ShapeDtypeStruct((3, 2, 8, 1, PAD), F32),
         ),
-        in_specs=[hbm, hbm, hbm, smem, smem, vmem, vmem, vmem],
+        in_specs=[hbm, hbm, hbm, smem, smem, hbm, hbm, hbm],
         out_specs=(hbm, hbm),
         scratch_shapes=[
             pltpu.VMEM((8, 10, 8, SEG), F32),
@@ -571,25 +616,34 @@
             pltpu.VMEM((2, 4, 8, 16, PAD), F32),
             pltpu.VMEM((8, 10, 1, PAD), F32),
             pltpu.VMEM((2, 4, 8, 1, PAD), F32),
+            pltpu.VMEM((2, 2, 48, 128), F32),
+            pltpu.VMEM((2, 2, 2, 32, 128), F32),
+            pltpu.VMEM((2, 3, 2, 2, 1, PAD), F32),
+            dma((4,)),
             dma((4, 8)), dma((4, 8)), dma, dma, dma((2, 2, 3)), dma((2, 2, 3)), dma((2, 2, 2)), dma((2, 2, 2)),
             dma((4, 8)), dma((4, 8)), dma((4, 8)), dma((4, 2)), dma((8,)),
         ],
         compiler_params=pltpu.CompilerParams(has_side_effects=True, collective_id=0, vmem_limit_bytes=60 * 1024 * 1024),
     )(wind_u, wind_v, tracer, cutoff, row_scale, coarse, fine, twiddle)
-    level = pl.BlockSpec((4, 64, SEG), lambda k: (k, 0, 0))
     shape = jax.ShapeDtypeStruct((8, 64, SEG), F32)
     return pl.pallas_call(
         stencil_kernel,
         name="flux_stencil",
-        grid=(2,),
         out_shape=(shape, shape, shape),
-        in_specs=[
-            pl.BlockSpec((3, 4, 64, PAD), lambda k: (0, k, 0, 0)),
-            pl.BlockSpec((3, 2, 4, 1, PAD), lambda k: (0, 0, k, 0, 0)),
-            level, smem,
+        in_specs=[hbm, hbm, hbm, smem],
+        out_specs=(hbm, hbm, hbm),
+        scratch_shapes=[
+            pltpu.VMEM((3, 8, 64, PAD), F32),
+            pltpu.VMEM((3, 2, 8, 1, PAD), F32),
+            pltpu.VMEM((8, 64, SEG), F32),
+            pltpu.VMEM((8, 64, SEG), F32),
+            pltpu.VMEM((8, 64, SEG), F32),
+            pltpu.VMEM((8, 64, SEG), F32),
+            pltpu.VMEM((64, LANES), F32),
+            pltpu.VMEM((64, LANES), F32),
+            dma((8, 5)), dma,
         ],
-        out_specs=(level, level, level),
-        scratch_shapes=[pltpu.VMEM((64, LANES), F32), pltpu.VMEM((64, LANES), F32)],
+        compiler_params=pltpu.CompilerParams(vmem_limit_bytes=60 * 1024 * 1024),
     )(filt, edge, tracer, row_scale)
 
 

time: 104 us -> 103 us (level)
  no operation moved by 1% of the time
where the time goes in v4:
time: 103 us
  Pallas kernels  102 us (99%)
    pallas_call x1, Pallas kernels, on_device(): pl.pallas_call(filter_kernel, name='polar_filter', out_shape=(jax.ShapeDt...  96.2 us
    pallas_call x1, Pallas kernels, on_device(): pl.pallas_call(stencil_kernel, name='flux_stencil', out_shape=(shape, sha...  6.05 us

profile of v4, /device:TPU:31, one launch (start us, length us, event | category | flops | bytes accessed | tf_op | source)
XLA Modules:
  0.0 103.1 jit_solution(6728711602814724438)
XLA Ops:
  0.6 96.2 %polar_filter.1 = (f32[3,8,64,768]{3,2,1,0:T(8,128)}, f32[3,2,8,1,768]{4,3,2,1,0:T(1,128)}) custom-call(f32[8,64,750]{2,1,0:T(8,128)} %u_ref.1, f32[8,64,750]{2,1,0:T(8,128)} %v_ref.1, f32[8,64,750]{2,1,0:T(8,128)} %tracer_far.1, s32[64]{0:T(128)} %cut_ref.1, f32[64]{0:T(128)} %row_scale_ref.1, f32[2,2,48,128]{3,2,1,0:T(8,128)} %constant.6.clone.coarse_far, ...), custom_call_target="tpu_custom_call" | custom-call | tf_op jit(solution)/shard_map/polar_filter/pallas_call | solution.py:592
  96.8 6.0 %flux_stencil.1 = (f32[8,64,750]{2,1,0:T(8,128)}, f32[8,64,750]{2,1,0:T(8,128)}, f32[8,64,750]{2,1,0:T(8,128)}) custom-call(f32[3,8,64,768]{3,2,1,0:T(8,128)} %get-tuple-element.5.filt_far, f32[3,2,8,1,768]{4,3,2,1,0:T(1,128)} %get-tuple-element.6.edge_far, f32[8,64,750]{2,1,0:T(8,128)} %tracer_far.1, f32[64]{0:T(128)} %row_scale_ref.1), custom_call_target="tpu_custom_call" | custom-call | tf_op jit(solution)/shard_map/flux_stencil/pallas_call | solution.py:629

commit v5 on v4

--- a/solution.py
+++ b/solution.py
@@ -218,7 +218,7 @@
     upper = 8 * either(me % 8 == 0) + 4 * either(half + core == 0)
     pl.semaphore_wait(barrier, 9 + lower * either(lat < 7) + upper * either(lat > 0))
 
-    for f in (1, 0, 3, 2):
+    for f in (0, 3, 1, 2):
         own_gather(f).start()
         each(1, count(f), lambda i, f=f: gather(f, i).start())
 
@@ -478,7 +478,7 @@
     send_back(2)
 
     swap().wait_send()
-    for f in (1, 0, 3, 2):
+    for f in (0, 3, 1, 2):
         own_scatter(f).wait()
         if not column(f):
             for d in range(2):

time: 103 us -> 103 us (level)
  no operation moved by 1% of the time
where the time goes in v5:
time: 103 us
  Pallas kernels  102 us (99%)
    pallas_call x1, Pallas kernels, on_device(): pl.pallas_call(filter_kernel, name='polar_filter', out_shape=(jax.ShapeDt...  96.2 us
    pallas_call x1, Pallas kernels, on_device(): pl.pallas_call(stencil_kernel, name='flux_stencil', out_shape=(shape, sha...  6.05 us

profile of v5, /device:TPU:31, one launch (start us, length us, event | category | flops | bytes accessed | tf_op | source)
XLA Modules:
  0.0 103.1 jit_solution(8555145676497389437)
XLA Ops:
  0.6 96.2 %polar_filter.1 = (f32[3,8,64,768]{3,2,1,0:T(8,128)}, f32[3,2,8,1,768]{4,3,2,1,0:T(1,128)}) custom-call(f32[8,64,750]{2,1,0:T(8,128)} %u_ref.1, f32[8,64,750]{2,1,0:T(8,128)} %v_ref.1, f32[8,64,750]{2,1,0:T(8,128)} %tracer_far.1, s32[64]{0:T(128)} %cut_ref.1, f32[64]{0:T(128)} %row_scale_ref.1, f32[2,2,48,128]{3,2,1,0:T(8,128)} %constant.6.clone.coarse_far, ...), custom_call_target="tpu_custom_call" | custom-call | tf_op jit(solution)/shard_map/polar_filter/pallas_call | solution.py:592
  96.8 6.0 %flux_stencil.1 = (f32[8,64,750]{2,1,0:T(8,128)}, f32[8,64,750]{2,1,0:T(8,128)}, f32[8,64,750]{2,1,0:T(8,128)}) custom-call(f32[3,8,64,768]{3,2,1,0:T(8,128)} %get-tuple-element.5.filt_far, f32[3,2,8,1,768]{4,3,2,1,0:T(1,128)} %get-tuple-element.6.edge_far, f32[8,64,750]{2,1,0:T(8,128)} %tracer_far.1, f32[64]{0:T(128)} %row_scale_ref.1), custom_call_target="tpu_custom_call" | custom-call | tf_op jit(solution)/shard_map/flux_stencil/pallas_call | solution.py:629
